TPU v7x, 128 devices: a whole 4x4x4 slice. The times are simulated.
128 devices in a mesh: lat: 8 (over x, core), lon: 16 (over y, z).
Axes of the slice: x: 4, y: 4, z: 4, core: 2. Of those that a mesh axis runs over, the one named last changes fastest.
Arguments:
- tracers: float32 [1024, 1152, 256], P(('lat', 'lon')), may hold values from 0.1 to 3
- phys_fine: bfloat16 [384, 6144, 144], P('lat', 'lon'), may hold values from -2 to 30, as said below
- mix_coarse: bfloat16 [128, 2048, 48], P('lat', 'lon'), may hold values from 0.0049743652 to 0.19921875
- surf_light: float32 [384, 6144], P('lat', 'lon'), may hold values from 0.5 to 4
- land_mask: int32 [128, 2048], P('lat', 'lon'), may hold values from 0 to 1, as said below
- owner_map: int32 [8, 128], P('lat'), may hold values from -1 to 1023, as said below
Outputs:
- tracers_out: float32 [1024, 1152, 256], P(('lat', 'lon'))
- heating: bfloat16 [48, 384, 6144], P(None, 'lat', 'lon')
Inputs may be any that keep to these rules, and one draw needn't show every extreme that they name: `owner_map`: -1 marks a block whose columns are all land, any other value is the slot that holds the block. Slots are numbered band by band, 128 to a band, owner by owner within a band with 8 slots each, and a block's slot lies in its own band. Every band has a multiple of 16 wet blocks. The wet blocks of a band, taken in order of longitude, are held by the owners in turn: the next wet block after one held by owner o is held by owner o + 1 (after 16 - 1 comes 0), also from the band's last wet block to its first; the r-th wet block of a band (from 0) lies in slot r // 16 of its owner. In some band every slot holds a block. `land_mask`: 1 for an ocean column, 0 for land; every column of a block that owner_map marks -1 is land. `phys_fine`: channel c * 48 + l holds level l of: c = 0 the eastward velocity on a fine cell's east face and c = 1 the northward velocity on its north face, as fractions of a cell per step within -0.15 to 0.15; c = 2 temperature within -2 to 30.
All inputs are finite; a program needn't handle non-finite values.
Results may differ from a plain program's by a relative error of at most 0.001.
Values sent between devices are 32-bit elements; how exact they have to be, the bound alone decides.
A program may use at most 192 MiB of HBM per device.

v0:
```python
import functools

import jax
import jax.numpy as jnp
from jax import lax
from jax.experimental import pallas as pl
from jax.experimental.pallas import tpu as pltpu
from jax.sharding import PartitionSpec as P

NTR = 24
LEV = 48
SIDE = 16
CELLS = 256
SLOTS = 8
TILE = 8
PHYS = 224
DIFF = 0.08
VM = pltpu.VMEM
ROWS3 = 3 * LEV
HALF = ROWS3 // 2


def pos(v):
    return jnp.maximum(v, 0.0)


def lanes():
    return lax.broadcasted_iota(jnp.int32, (LEV, 128), 1)


def roll(x, shift):
    return pltpu.roll(x, shift, 1)


def pack_edges(c_ref, rows_ref, w_ref, e_ref, odd):
    lane = lanes()
    group = lane // SIDE
    col = lane % SIDE
    low = lane < SIDE
    for m in range(3):
        blank = jnp.zeros((LEV, 128), jnp.float32)
        ends = [blank, blank]
        both = [blank, blank]
        for g in range(8):
            t = 3 * g + m
            a = c_ref[0, t * LEV:(t + 1) * LEV, 0:128]
            b = c_ref[0, t * LEV:(t + 1) * LEV, 128:256]
            end = jnp.where(low, a, b)
            ends[g % 2] = jnp.where((group == g) | (group == (g + 7) % 8), roll(end, 16 * g) if g else end, ends[g % 2])
            here = (col == 2 * g) | (col == (2 * g + 15) % 16)
            for h, v in enumerate((a, b)):
                both[h] = jnp.where(here, roll(v, 2 * g) if g else v, both[h])
        flat = group % 2 == 0
        put_rows(rows_ref, 0, m, jnp.where(flat, ends[0], ends[1]))
        put_rows(rows_ref, 1, m, jnp.where(flat, ends[1], ends[0]))
        at = slice(m * LEV, (m + 1) * LEV)
        mine = (lane % 2) == odd
        for h in range(2):
            hs = slice(h * 128, (h + 1) * 128)
            turned = roll(both[h], odd)
            w_ref[0, at, hs] = jnp.where(mine, turned, w_ref[0, at, hs])
            e_ref[0, at, hs] = jnp.where(mine, e_ref[0, at, hs], turned)


def put_rows(rows_ref, d, m, x):
    lo = m * LEV
    if lo < HALF:
        n = min(LEV, HALF - lo)
        rows_ref[0, 0, d, lo:lo + n, :] = x[:n]
        if n < LEV:
            rows_ref[0, 1, d, 0:LEV - n, :] = x[n:]
    else:
        rows_ref[0, 1, d, lo - HALF:lo - HALF + LEV, :] = x


def clear_first(odd, *refs):
    @pl.when(odd == 0)
    def _():
        for ref in refs:
            ref[...] = jnp.zeros_like(ref)


def pack_kernel(tab, c_ref, rows_ref, w_ref, e_ref):
    p = pl.program_id(0)
    lane = lanes()
    group = lane // SIDE
    col = lane % SIDE
    even = lane % 2 == 0
    low = lane < SIDE
    flat = group % 2 == 0
    for m in range(3):
        at = slice(m * LEV, (m + 1) * LEV)
        blank = jnp.zeros((LEV, 128), jnp.float32)
        both = [[blank, blank], [blank, blank]]
        for i in range(2):
            ends = [blank, blank]
            for g in range(8):
                t = 3 * g + m
                a = c_ref[i, t * LEV:(t + 1) * LEV, 0:128]
                b = c_ref[i, t * LEV:(t + 1) * LEV, 128:256]
                end = jnp.where(low, a, b)
                ends[g % 2] = jnp.where((group == g) | (group == (g + 7) % 8), roll(end, 16 * g) if g else end, ends[g % 2])
                here = (col == 2 * g) | (col == (2 * g + 15) % 16)
                for h, v in enumerate((a, b)):
                    both[i][h] = jnp.where(here, roll(v, 2 * g) if g else v, both[i][h])
            view = rows_ref.at[pl.ds(tab[2 * p + i, 4], 1)]
            put_rows(view, 0, m, jnp.where(flat, ends[0], ends[1]))
            put_rows(view, 1, m, jnp.where(flat, ends[1], ends[0]))
        for h in range(2):
            hs = slice(h * 128, (h + 1) * 128)
            other = roll(both[1][h], 1)
            w_ref[0, at, hs] = jnp.where(even, both[0][h], other)
            e_ref[0, at, hs] = jnp.where(even, other, both[0][h])


def pack(tab, tracers):
    return pl.pallas_call(
        pack_kernel,
        grid_spec=pltpu.PrefetchScalarGridSpec(
            num_scalar_prefetch=1,
            grid=(SLOTS // 2,),
            in_specs=[pl.BlockSpec((2, NTR * LEV, CELLS), lambda j, tab: (j, 0, 0))],
            out_specs=[
                pl.BlockSpec((8, 2, 2, HALF, 128), lambda j, tab: (0, 0, 0, 0, 0)),
                pl.BlockSpec((1, ROWS3, CELLS), lambda j, tab: (j, 0, 0)),
                pl.BlockSpec((1, ROWS3, CELLS), lambda j, tab: (j, 0, 0)),
            ],
        ),
        out_shape=[
            jax.ShapeDtypeStruct((8, 2, 2, HALF, 128), jnp.float32),
            jax.ShapeDtypeStruct((4, ROWS3, CELLS), jnp.float32),
            jax.ShapeDtypeStruct((4, ROWS3, CELLS), jnp.float32),
        ],
        cost_estimate=pl.CostEstimate(flops=10**7, bytes_accessed=12 * 10**6, transcendentals=0),
        name="pack",
    )(tab, tracers)


def react(get, put, par, warm):
    (carbon_dis, alkalinity, oxygen, nitrate, ammonium, phosphate, silicate, iron_free,
     nano_carbon, diat_carbon, nano_chl, diat_chl, nano_iron, diat_iron, diat_silica,
     micro_zoo, meso_zoo, dissolved_org, small_part, big_part, small_iron, big_iron,
     big_silica, calcite) = [functools.partial(get, t) for t in range(NTR)]
    p_am = pos(ammonium())
    nitrogen = pos(nitrate()) + p_am
    limit_nitro = nitrogen / (0.5 + nitrogen)
    p_ph = pos(phosphate())
    p_fe = pos(iron_free())
    p_si = pos(silicate())
    nutr_nano = jnp.minimum(jnp.minimum(limit_nitro, p_ph / (0.3 + p_ph)), p_fe / (0.2 + p_fe))
    nutr_diat = jnp.minimum(nutr_nano, p_si / (1.0 + p_si))
    nc = nano_carbon()
    dc = diat_carbon()
    wp = warm * par
    prod_nano = 0.1 * wp / (par + 0.5) * nutr_nano * nc
    prod_diat = 0.12 * wp / (par + 1.0) * nutr_diat * dc
    share = (p_am + 0.01) / (nitrogen + 0.02)
    mi = micro_zoo()
    me = meso_zoo()
    graze_nano = 0.08 * warm * mi / (1.0 + pos(nc))
    graze_diat = 0.06 * warm * me / (1.0 + pos(dc))
    loss_nano = graze_nano + 0.02
    loss_diat = graze_diat + 0.02
    eaten_nano = graze_nano * nc
    eaten_diat = graze_diat * dc
    death_micro = 0.03 * mi * pos(mi)
    death_meso = 0.03 * me * pos(me)
    do = dissolved_org()
    sp = small_part()
    bp = big_part()
    remin_doc = 0.03 * warm * do
    remin_poc = 0.02 * warm * sp
    remin_goc = 0.01 * warm * bp
    am = ammonium()
    nitrify = 0.05 * am
    cal = calcite()
    melt_cal = 0.01 * cal
    uptake = prod_nano + prod_diat
    remin = remin_doc + remin_poc + remin_goc
    calcify = 0.02 * prod_nano
    shell = melt_cal - calcify
    put(0, carbon_dis() + remin - uptake + shell)
    su = share * uptake
    fresh = uptake - su
    put(1, alkalinity() + 2.0 * shell + 0.16 * (fresh - nitrify))
    put(2, oxygen() + 1.3 * (uptake - remin) - 0.32 * nitrify)
    put(3, nitrate() + 0.16 * (nitrify - fresh))
    put(4, am + 0.16 * (remin - su - nitrify))
    put(5, phosphate() + 0.01 * (remin - uptake))
    bsi = big_silica()
    melt_si = 0.02 * bsi
    put(6, silicate() + melt_si - 0.15 * prod_diat)
    sfe = small_iron()
    bfe = big_iron()
    melt_sfe = 0.02 * sfe
    melt_bfe = 0.01 * bfe
    put(7, iron_free() + melt_sfe + melt_bfe - 0.005 * uptake)
    put(8, nc + prod_nano - loss_nano * nc)
    put(9, dc + prod_diat - loss_diat * dc)
    x = nano_chl()
    put(10, x + 0.03 * prod_nano - loss_nano * x)
    x = diat_chl()
    put(11, x + 0.03 * prod_diat - loss_diat * x)
    x = nano_iron()
    lost = loss_nano * x
    put(12, x + 0.005 * prod_nano - lost)
    put(20, sfe + lost - melt_sfe)
    x = diat_iron()
    lost = loss_diat * x
    put(13, x + 0.005 * prod_diat - lost)
    put(21, bfe + lost - melt_bfe)
    x = diat_silica()
    lost = loss_diat * x
    put(14, x + 0.15 * prod_diat - lost)
    put(22, bsi + lost - melt_si)
    put(15, mi + 0.3 * eaten_nano - death_micro)
    put(16, me + 0.3 * eaten_diat - death_meso)
    put(17, do + 0.3 * eaten_nano + 0.02 * nc - remin_doc)
    put(18, sp + 0.4 * eaten_nano + death_micro - remin_poc)
    put(19, bp + 0.4 * eaten_diat + 0.02 * dc + death_meso - remin_goc)
    put(23, cal - shell)


def tri():
    i = lax.broadcasted_iota(jnp.int32, (LEV, LEV), 0)
    j = lax.broadcasted_iota(jnp.int32, (LEV, LEV), 1)
    return (j < i).astype(jnp.float32)


def depth(absorb):
    return jnp.dot(tri(), absorb, precision=lax.Precision.HIGHEST,
                   preferred_element_type=jnp.float32)


def slot_step(tab, c_ref, phys, rows, west, east, out, coef, par_ref, cross, along, one, two):
    j = pl.program_id(0)
    w_odd = tab[j, 0] % 2
    e_odd = tab[j, 1] % 2
    lane = lanes()
    col = lane % SIDE
    at_w = col == 0
    at_e = col == SIDE - 1
    low = lane < 16
    high = lane >= 112
    H = (slice(0, 128), slice(128, 256))
    edge = jnp.concatenate([phys[0, 200:224, 0:128], phys[0, 200:224, 128:256]], axis=0)
    sel_r = lax.broadcasted_iota(jnp.int32, (128, 256), 0)
    sel_c = lax.broadcasted_iota(jnp.int32, (128, 256), 1)
    sel = ((sel_c == SIDE * sel_r) & (sel_r < SIDE)).astype(jnp.float32)
    edge_lane = jnp.where(low, edge, 0.0)
    edge_w = jnp.dot(edge_lane, sel, precision=lax.Precision.HIGHEST,
                     preferred_element_type=jnp.float32)
    edge_s = roll(edge, 112)
    fn_up = roll(phys[0, 48:96, H[0]], 16)
    level = lax.broadcasted_iota(jnp.int32, (LEV, 128), 0)
    for h in range(2):
        fe = phys[0, 0:48, H[h]]
        fn = phys[0, 48:96, H[h]]
        fw = jnp.where(at_w, edge_w[:, H[h]], roll(fe, 1))
        if h == 0:
            fs = jnp.where(low, edge_s, fn_up)
        else:
            fs = jnp.where(low, fn_up, roll(fn, 16))
        ow = DIFF * phys[0, 192:193, H[h]]
        oe = DIFF * phys[0, 193:194, H[h]]
        os = DIFF * phys[0, 194:195, H[h]]
        on = DIFF * phys[0, 195:196, H[h]]
        coef[0, :, H[h]] = (1.0 - (ow + oe + os + on)) - pos(fe) + jnp.minimum(fw, 0.0) - pos(fn) + jnp.minimum(fs, 0.0)
        coef[1, :, H[h]] = oe - jnp.minimum(fe, 0.0)
        coef[2, :, H[h]] = ow + pos(fw)
        coef[3, :, H[h]] = on - jnp.minimum(fn, 0.0)
        coef[4, :, H[h]] = os + pos(fs)
        below = jnp.where(level < LEV - 1, phys[0, 144:192, H[h]], 0.0)
        coef[5, :, H[h]] = below

    wide = lax.broadcasted_iota(jnp.int32, (HALF, 128), 1)
    flat = (wide // SIDE) % 2 == 0
    for p in range(2):
        hp = slice(p * HALF, (p + 1) * HALF)
        upper = rows[0, p, 1, :, :]
        under = roll(rows[0, p, 0, :, :], 32)
        cross[0, hp, :] = jnp.where(flat, upper, under)
        cross[1, hp, :] = jnp.where(flat, under, upper)
        for h in range(2):
            along[hp, H[h]] = jnp.where(wide % 2 == 0, roll(west[0, hp, H[h]], 128 - 15 - w_odd),
                                        roll(east[0, hp, H[h]], 15 - e_odd))

    def where(g, m):
        return pl.ds(pl.multiple_of((3 * g + m) * LEV, LEV), LEV)

    def turn_to(g, m, around):
        hm = slice(m * LEV, (m + 1) * LEV)
        a = c_ref[0, where(g, m), H[0]]
        b = c_ref[0, where(g, m), H[1]]
        ends = roll(cross[lax.rem(g, 2), hm, :], 112 - 16 * g)
        an, bn = roll(a, 112), roll(b, 112)
        as_, bs = roll(a, 16), roll(b, 16)
        around[m, 0, :, H[0]] = jnp.where(high, bn, an)
        around[m, 0, :, H[1]] = jnp.where(high, ends, bn)
        around[m, 1, :, H[0]] = jnp.where(low, ends, as_)
        around[m, 1, :, H[1]] = jnp.where(low, as_, bs)
        for h, v in enumerate((a, b)):
            sides = roll(along[hm, H[h]], lax.rem(128 - 2 * g, 128))
            around[m, 2, :, H[h]] = jnp.where(at_w, sides, roll(v, 1))
            around[m, 3, :, H[h]] = jnp.where(at_e, sides, roll(v, 127))

    def move(g, m, around):
        for h in range(2):
            v = c_ref[0, where(g, m), H[h]]
            moved = (coef[0, :, H[h]] * v + coef[1, :, H[h]] * around[m, 3, :, H[h]]
                     + coef[2, :, H[h]] * around[m, 2, :, H[h]]
                     + coef[3, :, H[h]] * around[m, 0, :, H[h]] + coef[4, :, H[h]] * around[m, 1, :, H[h]])
            flux = coef[5, :, H[h]] * (pltpu.roll(moved, LEV - 1, 0) - moved)
            out[0, where(g, m), H[h]] = moved + flux - pltpu.roll(flux, 1, 0)

    for m in range(3):
        turn_to(0, m, one)

    def pair(i, carry):
        for now, then, g in ((one, two, 2 * i), (two, one, 2 * i + 1)):
            for m in range(3):
                move(g, m, now)
                turn_to(jnp.minimum(g + 1, 7), m, then)
        return carry

    lax.fori_loop(0, 4, pair, 0)
    absorb = 0.04 + 0.02 * (pos(out[0, 480:528, :]) + pos(out[0, 528:576, :]))
    above = depth(absorb)
    par_ref[...] = phys[0, 196:197, :] * jnp.exp(-(above + 0.5 * absorb))
    for h in range(2):
        wet = jnp.broadcast_to(phys[0, 197:198, H[h]], (8, 128))

        def chunk(i, carry):
            l0 = pl.multiple_of(i * 8, 8)

            def get(t):
                return out[0, pl.ds(pl.multiple_of(t * LEV + l0, 8), 8), H[h]]

            held = [get(t) for t in range(NTR)]

            def put(t, v):
                out[0, pl.ds(pl.multiple_of(t * LEV + l0, 8), 8), H[h]] = v * wet

            warm = jnp.exp(0.0639 * phys[0, pl.ds(pl.multiple_of(96 + l0, 8), 8), H[h]])
            par = par_ref[pl.ds(l0, 8), H[h]]
            react(lambda t: held[t], put, par, warm)
            return carry

        lax.fori_loop(0, LEV // 8, chunk, 0)


def first_kernel(tab, c_ref, phys, rows, west, east, out, rows_out, w_out, e_out, coef, par_ref, cross, along, one, two):
    j = pl.program_id(0)
    odd = j % 2

    @pl.when(tab[j, 2] == 1)
    def _():
        slot_step(tab, c_ref, phys, rows, west, east, out, coef, par_ref, cross, along, one, two)

    @pl.when(tab[j, 2] == 0)
    def _():
        out[...] = jnp.zeros_like(out)

    clear_first(odd, w_out, e_out)
    pack_edges(out, rows_out, w_out, e_out, odd)


def last_kernel(tab, c_ref, phys, rows, west, east, out, light_out, coef, par_ref, cross, along, one, two):
    j = pl.program_id(0)

    @pl.when(tab[j, 2] == 1)
    def _():
        slot_step(tab, c_ref, phys, rows, west, east, out, coef, par_ref, cross, along, one, two)
        absorb = 0.04 + 0.02 * (pos(out[0, 480:528, :]) + pos(out[0, 528:576, :]))
        above = depth(absorb)
        light_out[0] = jnp.exp(-above) - jnp.exp(-(above + absorb))

    @pl.when(tab[j, 2] == 0)
    def _():
        out[...] = jnp.zeros_like(out)
        light_out[...] = jnp.zeros_like(light_out)


def step(last, tab, current, phys, rows, came_west, came_east):
    edge_spec = pl.BlockSpec((1, ROWS3, CELLS), lambda j, tab: (j // 2, 0, 0))
    edge_shape = jax.ShapeDtypeStruct((4, ROWS3, CELLS), jnp.float32)
    if last:
        outs = [pl.BlockSpec((1, LEV, CELLS), lambda j, tab: (tab[j, 5], 0, 0))]
        shapes = [jax.ShapeDtypeStruct((16, LEV, CELLS), jnp.float32)]
    else:
        outs = [pl.BlockSpec((1, 2, 2, HALF, 128), lambda j, tab: (tab[j, 4], 0, 0, 0, 0)), edge_spec, edge_spec]
        shapes = [jax.ShapeDtypeStruct((8, 2, 2, HALF, 128), jnp.float32), edge_shape, edge_shape]
    return pl.pallas_call(
        last_kernel if last else first_kernel,
        grid_spec=pltpu.PrefetchScalarGridSpec(
            num_scalar_prefetch=1,
            grid=(SLOTS,),
            in_specs=[
                pl.BlockSpec((1, NTR * LEV, CELLS), lambda j, tab: (j, 0, 0)),
                pl.BlockSpec((1, PHYS, CELLS), lambda j, tab: (tab[j, 8], 0, 0)),
                pl.BlockSpec((1, 2, 2, HALF, 128), lambda j, tab: (tab[j, 3], 0, 0, 0, 0)),
                pl.BlockSpec((1, ROWS3, CELLS), lambda j, tab: (tab[j, 0] // 2, 0, 0)),
                pl.BlockSpec((1, ROWS3, CELLS), lambda j, tab: (tab[j, 1] // 2, 0, 0)),
            ],
            out_specs=[pl.BlockSpec((1, NTR * LEV, CELLS), lambda j, tab: (j, 0, 0))] + outs,
            scratch_shapes=[VM((6, LEV, CELLS), jnp.float32), VM((LEV, CELLS), jnp.float32),
                            VM((2, ROWS3, 128), jnp.float32), VM((ROWS3, CELLS), jnp.float32),
                            VM((3, 4, LEV, CELLS), jnp.float32), VM((3, 4, LEV, CELLS), jnp.float32)],
        ),
        out_shape=[jax.ShapeDtypeStruct((SLOTS, NTR * LEV, CELLS), jnp.float32)] + shapes,
        cost_estimate=pl.CostEstimate(flops=10**8, bytes_accessed=25 * 10**6, transcendentals=10**6),
        name="last_step" if last else "first_step",
    )(tab, current, phys, rows, came_west, came_east)


def spread_matrix(shape, lhs_wide, dtype=jnp.bfloat16):
    i = lax.broadcasted_iota(jnp.int32, shape, 0)
    j = lax.broadcasted_iota(jnp.int32, shape, 1)
    return (i // 3 == j if lhs_wide else i == j // 3).astype(dtype)


def coarse_kernel(phys, mix, flags, y_ref, col_ref, every_ref, third_ref):
    step = pl.program_id(0)

    @pl.when(step == 0)
    def _():
        i = lax.broadcasted_iota(jnp.int32, (384, 128), 0)
        j = lax.broadcasted_iota(jnp.int32, (384, 128), 1)
        every_ref[...] = (i // 3 == j).astype(jnp.bfloat16)
        third_ref[...] = (i == 3 * j + 2).astype(jnp.bfloat16)
        col_ref[...] = jnp.zeros_like(col_ref)

    def dot(a, b):
        return jnp.dot(a, b, preferred_element_type=jnp.float32)

    u = jnp.concatenate([phys[f, 0:48, :] for f in range(6)], axis=0)
    vt = jnp.concatenate([phys[2, 48:96, :], phys[5, 48:96, :]] + [phys[f, 96:144, :] for f in range(6)], axis=0)
    east = dot(u, third_ref[...])
    rest = dot(vt, every_ref[...])

    def part(x, n):
        return x[48 * n:48 * n + 48]

    for c in range(2):
        e = (part(east, 3 * c) + part(east, 3 * c + 1) + part(east, 3 * c + 2)) / 3.0 * flags[c, 1:2, :]
        y_ref[c, 0:48, :] = e
        y_ref[c, 48:96, :] = part(rest, c) / 3.0 * flags[c, 3:4, :]
        y_ref[c, 96:144, :] = (part(rest, 3 * c + 2) + part(rest, 3 * c + 3) + part(rest, 3 * c + 4)) / 9.0
        y_ref[c, 144:192, :] = mix[c].astype(jnp.float32)
        y_ref[c, 192:200, :] = flags[c]
        r = 2 * step + c
        col_ref[...] = jnp.where(lanes() == r, roll(e, r + 1), col_ref[...])


def coarse(phys_t, mix_t, flags):
    return pl.pallas_call(
        coarse_kernel,
        grid=(SIDE // 2,),
        in_specs=[
            pl.BlockSpec((6, 144, 384), lambda r: (r, 0, 0)),
            pl.BlockSpec((2, LEV, 128), lambda r: (r, 0, 0)),
            pl.BlockSpec((2, 8, 128), lambda r: (r, 0, 0)),
        ],
        out_specs=[
            pl.BlockSpec((2, 200, 128), lambda r: (r, 0, 0)),
            pl.BlockSpec((LEV, 128), lambda r: (0, 0)),
        ],
        out_shape=[
            jax.ShapeDtypeStruct((SIDE, 200, 128), jnp.float32),
            jax.ShapeDtypeStruct((LEV, 128), jnp.float32),
        ],
        scratch_shapes=[VM((384, 128), jnp.bfloat16), VM((384, 128), jnp.bfloat16)],
        cost_estimate=pl.CostEstimate(flops=10**9, bytes_accessed=8 * 10**6, transcendentals=0),
        name="coarse",
    )(phys_t, mix_t, flags)


def package_kernel(tab, y_ref, col_ref, row_ref, out):
    group = lax.broadcasted_iota(jnp.int32, (8, 128), 1) // SIDE

    def chunk(i, carry):
        at = pl.ds(pl.multiple_of(8 * i, 8), 8)
        for h in range(2):
            vals = [y_ref[8 * h + g, at, :] for g in range(8)]
            for d in (1, 2, 4):
                lower = (group // d) % 2 == 0
                for g in range(8):
                    if g & d:
                        continue
                    a, b = vals[g], vals[g + d]
                    vals[g] = jnp.where(lower, a, roll(b, 16 * d))
                    vals[g + d] = jnp.where(lower, roll(a, 128 - 16 * d), b)
            for k in range(TILE):
                out[tab[k, 7], at, 128 * h:128 * h + 128] = vals[k]
        return carry

    lax.fori_loop(0, 25, chunk, 0)
    i = lax.broadcasted_iota(jnp.int32, (256, 128), 0)
    j = lax.broadcasted_iota(jnp.int32, (256, 128), 1)
    last = (i == SIDE * j + SIDE - 1).astype(jnp.float32)
    low = lanes() < SIDE
    for k in range(TILE):
        if k:
            west = jnp.dot(out[tab[k - 1, 7], 0:48, :], last, precision=lax.Precision.HIGHEST,
                           preferred_element_type=jnp.float32)
        else:
            west = col_ref[...]
        edge = jnp.where(low, west, roll(row_ref[...], (16 - 16 * k) % 128))
        out[tab[k, 7], 200:224, 0:128] = edge[0:24]
        out[tab[k, 7], 200:224, 128:256] = edge[24:48]


def package(tab, y, col, row):
    return pl.pallas_call(
        package_kernel,
        in_specs=[pl.BlockSpec(memory_space=pltpu.SMEM)] + [pl.BlockSpec(memory_space=VM)] * 3,
        out_specs=pl.BlockSpec(memory_space=VM),
        out_shape=jax.ShapeDtypeStruct((8, PHYS, CELLS), jnp.float32),
        cost_estimate=pl.CostEstimate(flops=10**7, bytes_accessed=4 * 10**6, transcendentals=0),
        name="package",
    )(tab, y, col, row)


MESH = pl.DeviceIdType.MESH


def remote(src, dst, send, recv, where):
    return pltpu.make_async_remote_copy(src_ref=src, dst_ref=dst, send_sem=send, recv_sem=recv,
                                        device_id=where, device_id_type=MESH)


PARTS = 4
PART = PHYS // PARTS
ORDER = (0, 5, 10, 15, 4, 1, 8, 2, 12, 3, 6, 9, 7, 13, 11, 14)


def each(first, last, fn):
    def body(d, carry):
        fn(d)
        return carry

    lax.fori_loop(first, last, body, 0)


def halo_kernel(first, *refs):
    if first:
        (tab, up_ref, phys, rows_ref, phys_out, got_s, got_n, pick, turn, mid0, mid1, mid2, mid3,
         up_send, up_recv, dn_send, dn_recv, z_send, z_recv, y_send, y_recv, own) = refs
        mid = (mid0, mid1, mid2, mid3)
    else:
        (tab, up_ref, w_ref, e_ref, rows_ref, from_w, from_e, got_s, got_n, pick,
         up_send, up_recv, dn_send, dn_recv, we_send, we_recv) = refs
    lat, lon = lax.axis_index("lat"), lax.axis_index("lon")
    bands, count = lax.axis_size("lat"), lax.axis_size("lon")
    sides = (lax.rem(lat + 1, bands), lax.rem(lat + bands - 1, bands))
    row, place = lon // 4, lax.rem(lon, 4)
    got = (got_s, got_n)
    barrier = pltpu.get_barrier_semaphore()

    def ahead(d):
        return lax.rem(row + d // 4, 4) * 4 + lax.rem(place + d % 4, 4)

    def behind(d):
        return lax.rem(row + 4 - d // 4, 4) * 4 + lax.rem(place + 4 - d % 4, 4)

    def greet(d):
        peer = lax.rem(lon + d, count)
        for side in sides:
            pl.semaphore_signal(barrier, inc=1, device_id=(side, peer), device_id_type=MESH)

    each(0, count, greet)
    each(1, count, lambda d: pl.semaphore_signal(
        barrier, inc=1, device_id=(lat, lax.rem(lon + d, count)), device_id_type=MESH))
    pl.semaphore_wait(barrier, 3 * count - 1)

    def up(n, d):
        peer = ahead(d)
        return remote(up_ref.at[peer, 1 - n], got[n].at[lon], up_send.at[n, d], up_recv.at[n, d], (sides[n], peer))

    def up_from(n, d):
        peer = behind(d)
        return remote(up_ref.at[peer, 1 - n], got[n].at[peer], up_send.at[n, d], up_recv.at[n, d], (sides[1 - n], peer))

    def down(n, d):
        peer = ahead(d)
        return remote(pick.at[n, peer], rows_ref.at[lon, n], dn_send.at[n, d], dn_recv.at[n, d], (lat, peer))

    def down_from(n, d):
        peer = behind(d)
        return remote(pick.at[n, peer], rows_ref.at[peer, n], dn_send.at[n, d], dn_recv.at[n, d], (lat, peer))

    def piece(p):
        return pl.ds(p * PART, PART)

    def by_z(p, d):
        z = lax.rem(place + d, 4)
        return remote(phys.at[z, :, piece(p)], mid[p].at[place], z_send.at[p, d], z_recv.at[p, d], (lat, 4 * row + z))

    def from_z(p, d):
        z = lax.rem(place + 4 - d, 4)
        return remote(phys.at[z, :, piece(p)], mid[p].at[z], z_send.at[p, d], z_recv.at[p, d], (lat, 4 * row + z))

    def by_y(p, d):
        y = lax.rem(row + d, 4)
        return remote(turn.at[y, :, piece(p)], phys_out.at[row, :, piece(p)], y_send.at[p, d], y_recv.at[p, d], (lat, 4 * y + place))

    def from_y(p, d):
        y = lax.rem(row + 4 - d, 4)
        return remote(turn.at[y, :, piece(p)], phys_out.at[y, :, piece(p)], y_send.at[p, d], y_recv.at[p, d], (lat, 4 * y + place))

    def lift(n):
        for d in ORDER:
            up(n, d).start()

    def descend(n):
        for d in ORDER:
            up_from(n, d).wait_recv()

        def choose(o):
            value = got[n][tab[o, 2 * n]]
            pick[n, o] = jnp.where(tab[o, 2 * n + 1] > 0, value, 0.0)

        each(0, count, choose)
        rows_ref[lon, n] = pick[n, lon]
        for d in ORDER[1:]:
            down(n, d).start()

    def stay(p):
        return pltpu.make_async_copy(phys.at[place, :, piece(p)], mid[p].at[place], own.at[p])

    def send_z(p):
        for d in (2, 1, 3):
            by_z(p, d).start()
        stay(p).start()

    def send_y(p):
        for d in (1, 2, 3):
            from_z(p, d).wait_recv()
        stay(p).wait()

        def sort(q):
            turn[q // 2, lax.rem(q, 2), piece(p)] = mid[p][tab[q, 4] // 2, lax.rem(tab[q, 4], 2)]

        each(0, 8, sort)
        for d in (2, 1, 3):
            by_y(p, d).start()
        phys_out[row, :, piece(p)] = turn[row, :, piece(p)]

    if first:
        send_z(0)
        lift(0)
        send_z(1)
        lift(1)
        send_z(2)
        send_z(3)
        send_y(0)
        descend(0)
        send_y(1)
        descend(1)
        send_y(2)
        send_y(3)
    else:
        to_e = remote(e_ref, from_w, we_send.at[0], we_recv.at[0], (lat, lax.rem(lon + 1, count)))
        to_w = remote(w_ref, from_e, we_send.at[1], we_recv.at[1], (lat, lax.rem(lon + count - 1, count)))
        lift(0)
        lift(1)
        descend(0)
        to_e.start()
        to_w.start()
        descend(1)
    for n in range(2):
        for d in ORDER[1:]:
            down_from(n, d).wait_recv()
    for n in range(2):
        for d in ORDER:
            up(n, d).wait_send()
        for d in ORDER[1:]:
            down(n, d).wait_send()
    if first:
        for p in range(PARTS):
            for d in (1, 2, 3):
                from_y(p, d).wait_recv()
                by_z(p, d).wait_send()
                by_y(p, d).wait_send()
    else:
        to_e.wait()
        to_w.wait()


def halo(first, tab, rows, *rest):
    anywhere = pl.BlockSpec(memory_space=pl.ANY)
    here = pl.BlockSpec(memory_space=VM)
    edge = jax.ShapeDtypeStruct((4, ROWS3, CELLS), jnp.float32)
    dma = pltpu.SemaphoreType.DMA
    sent = pltpu.VMEM((4, 2, PHYS, CELLS), jnp.float32)
    out = [jax.ShapeDtypeStruct((16, 2, HALF, 128), jnp.float32)]
    scratch = [VM((16, HALF, 128), jnp.float32), VM((16, HALF, 128), jnp.float32),
               VM((2, 16, HALF, 128), jnp.float32)]
    sems = [dma((2, 16)), dma((2, 16)), dma((2, 16)), dma((2, 16))]
    if first:
        in_specs, out_specs = [here], [here, here]
        out.append(jax.ShapeDtypeStruct((4, 2, PHYS, CELLS), jnp.float32))
        scratch += [sent] + [VM((4, 2, PART, CELLS), jnp.float32)] * PARTS
        scratch += sems + [dma((PARTS, 4))] * 4 + [dma((PARTS,))]
        rest = [rest[0].reshape(4, 2, PHYS, CELLS)]
    else:
        in_specs, out_specs = [anywhere] * 2, [here] + [anywhere] * 2
        out += [edge, edge]
        scratch += sems + [dma((2,)), dma((2,))]
    rows, *more = pl.pallas_call(
        functools.partial(halo_kernel, first),
        in_specs=[pl.BlockSpec(memory_space=pltpu.SMEM), here] + in_specs,
        out_specs=out_specs,
        out_shape=out,
        scratch_shapes=scratch,
        compiler_params=pltpu.CompilerParams(collective_id=1 if first else 2, has_side_effects=True),
        cost_estimate=pl.CostEstimate(flops=10**6, bytes_accessed=10**8, transcendentals=0),
        name="halo_phys" if first else "halo",
    )(tab, rows.reshape(16, 2, HALF, 128), *rest)
    return [rows.reshape(8, 2, 2, HALF, 128)] + more


def heat_kernel(tab, got, wet, light, out, fine):
    lane = lanes()
    group = lane // SIDE
    for r in range(SIDE):
        half = slice(128 * (r // 8), 128 * (r // 8) + 128)
        acc = jnp.zeros((LEV, 128), jnp.float32)
        for k in range(TILE):
            acc = jnp.where(group == k, roll(got[tab[k, 6], :, half], (16 * k - 16 * (r % 8)) % 128), acc)
        acc = jnp.where(wet[r:r + 1, :] > 0.0, acc, 0.0)
        for a in range(3):
            fine[pl.ds(3 * r + a, LEV, stride=LEV), :] = acc
    spread = spread_matrix((128, 384), False)
    stacked = jnp.concatenate([spread] * 3, axis=0)

    def levels(i, carry):
        x = fine[pl.ds(pl.multiple_of(i * 8 * LEV, 8 * LEV), 8 * LEV), :]
        high = x.astype(jnp.bfloat16)
        rest = x - high.astype(jnp.float32)
        mid = rest.astype(jnp.bfloat16)
        low = (rest - mid.astype(jnp.float32)).astype(jnp.bfloat16)
        wide = jnp.dot(jnp.concatenate([high, mid, low], axis=1), stacked,
                       preferred_element_type=jnp.float32)
        for l in range(8):
            out[8 * i + l] = (light[...] * wide[l * LEV:l * LEV + LEV]).astype(jnp.bfloat16)
        return carry

    lax.fori_loop(0, LEV // 8, levels, 0)


def heat(tab, got, wet, light):
    return pl.pallas_call(
        heat_kernel,
        in_specs=[pl.BlockSpec(memory_space=pltpu.SMEM)] + [pl.BlockSpec(memory_space=VM)] * 3,
        out_specs=pl.BlockSpec(memory_space=VM),
        out_shape=jax.ShapeDtypeStruct((LEV, 48, 384), jnp.bfloat16),
        scratch_shapes=[VM((LEV * LEV, 128), jnp.float32)],
        cost_estimate=pl.CostEstimate(flops=10**9, bytes_accessed=3 * 10**6, transcendentals=0),
        name="heat",
    )(tab, got, wet, light)


def prep_kernel(base, south, north, west, east, light, flags, tab, meet, sums):
    lat, lon = lax.axis_index("lat"), lax.axis_index("lon")
    wet = base[0:16, :]
    lane = lax.broadcasted_iota(jnp.int32, (SIDE, 128), 1)
    line = lax.broadcasted_iota(jnp.int32, (SIDE, 128), 0)
    wet_e = jnp.where(lane == 127, roll(east[0:16, :], 127), roll(wet, 127))
    wet_w = jnp.where(lane == 0, roll(west[0:16, :], 1), roll(wet, 1))
    inner_n = (lat < lax.axis_size("lat") - 1).astype(jnp.float32)
    inner_s = (lat > 0).astype(jnp.float32)
    wet_n = jnp.where(line == 15, inner_n * north[0:1, :], pltpu.roll(wet, 15, 0))
    wet_s = jnp.where(line == 0, inner_s * south[15:16, :], pltpu.roll(wet, 1, 0))
    sums[...] = jnp.dot(light[...], spread_matrix((384, 128), True, jnp.float32),
                        precision=lax.Precision.HIGHEST, preferred_element_type=jnp.float32)
    mean = sums[pl.ds(0, 16, stride=3), :] + sums[pl.ds(1, 16, stride=3), :] + sums[pl.ds(2, 16, stride=3), :]
    values = (wet * wet_w, wet * wet_e, wet * wet_s, wet * wet_n, mean / 9.0, wet,
              jnp.zeros_like(wet), jnp.zeros_like(wet))
    for i, v in enumerate(values):
        flags[pl.ds(i, 16, stride=8), :] = v

    def ints(ref):
        return ref[16:17, :].astype(jnp.int32)

    def owner_of(code):
        return lax.shift_right_arithmetic(code, 3) & 15

    def f32(x):
        return x.astype(jnp.float32)

    def wide(x, n):
        return jnp.broadcast_to(x, (n, 128))

    band = ints(base)
    big_i = lax.broadcasted_iota(jnp.int32, (128, 128), 0)
    big_j = lax.broadcasted_iota(jnp.int32, (128, 128), 1)
    down = jnp.sum(jnp.where(big_i == big_j, f32(wide(band, 128)), 0.0), axis=1, keepdims=True).astype(jnp.int32)
    down = jnp.broadcast_to(down, (128, 128))
    own_i, own_j = owner_of(down), owner_of(wide(band, 128))
    before = (big_i < big_j) & (down >= 0)
    near = jnp.sum(f32(before & (big_i // 8 == big_j // 8) & ((own_i & 3) == (own_j & 3))), axis=0, keepdims=True)
    far = jnp.sum(f32(before & (big_i // 32 == big_j // 32) & (own_i == own_j)), axis=0, keepdims=True)
    ids = lax.broadcasted_iota(jnp.int32, (1, 128), 1)
    own = owner_of(band)
    wet_b = band >= 0

    def total(mask, value):
        n = mask.shape[0]
        return jnp.sum(jnp.where(mask, wide(f32(value), n), 0.0), axis=1, keepdims=True)

    slot = lax.broadcasted_iota(jnp.int32, (8, 128), 0)
    ids8 = wide(ids, 8)
    band8 = wide(band, 8)
    hit = band8 == (lat * 16 + lon) * SLOTS + slot
    full = total(hit, jnp.ones_like(band))
    pair = total(hit, ids // 16)
    got_at = total(hit, ids // 32 * 2) + total(hit, far)
    west_code = total(hit, roll(band, 1))
    east_code = total(hit, roll(band, 127))

    def slot_of(code):
        code = code.astype(jnp.int32)
        return f32(jnp.where(code >= 0, code & 7, 0))

    w_slot, e_slot = slot_of(west_code), slot_of(east_code)
    some = jnp.broadcast_to(ids8 // 16 == slot, (8, 128))
    band_hit = wide(f32(jnp.max(f32(hit), axis=0, keepdims=True)), 8) > 0.0
    first_of = lax.broadcasted_iota(jnp.int32, (8, 1), 0).astype(jnp.float32)
    pair_used = total(some & band_hit, jnp.ones_like(band))
    pair_spare = jnp.min(jnp.where(pair_used > 0.0, 99.0, first_of), axis=0, keepdims=True)
    my_tile = ids // TILE == lon
    tile_mask = (ids8 // TILE == lon) & (ids8 - TILE * lon == slot)
    t_wet = total(tile_mask & (band8 >= 0), jnp.ones_like(band))
    t_own = total(tile_mask & (band8 >= 0), own)
    z_key = (own & 3) * 2 + near.astype(jnp.int32)
    z_at = total(tile_mask & (band8 >= 0), z_key)
    z_used = total(wide(my_tile & wet_b, 8) & (wide(z_key, 8) == slot), jnp.ones_like(band))
    z_spare = jnp.min(jnp.where(z_used > 0.0, 99.0, first_of), axis=0, keepdims=True)
    z_at = jnp.where(t_wet > 0.0, z_at, jnp.minimum(z_spare, 7.0))
    t_first = lax.broadcasted_iota(jnp.int32, (16, 1), 0).astype(jnp.float32)
    row16 = lax.broadcasted_iota(jnp.int32, (16, 128), 0)
    in_tile = wide(my_tile & wet_b, 16)
    to_me = jnp.max(f32(hit), axis=0, keepdims=True)
    src_used = total((wide(ids // TILE, 16) == row16) & (wide(to_me, 16) > 0.0), jnp.ones_like(band))
    src_spare = jnp.min(jnp.where(src_used > 0.0, 99.0, t_first), axis=0, keepdims=True)
    src = total(hit, ids // TILE)
    fields = (w_slot, e_slot, full, pair, jnp.where(full > 0.0, pair, jnp.minimum(pair_spare, 7.0)),
              jnp.where(full > 0.0, src, src_spare), t_own, z_at, got_at)
    acc = jnp.zeros((8, 128), jnp.float32)
    for i, v in enumerate(fields):
        acc = jnp.where(ids8 == i, v, acc)
    tab[...] = acc.astype(jnp.int32)
    ids16 = wide(ids, 16)
    here = (ids16 // 16 == lon // 2) & wide(wet_b, 16) & (wide(own, 16) == row16)
    acc = jnp.zeros((16, 128), jnp.float32)
    for i, other in enumerate((ints(south), ints(north))):
        both = here & (wide(other, 16) >= 0)
        acc = jnp.where(ids16 == 2 * i, total(both, owner_of(other)), acc)
        acc = jnp.where(ids16 == 2 * i + 1, total(both, jnp.ones_like(band)), acc)
    mine = wet_b & (ids // 32 == lon // 4) & ((own & 3) == lax.rem(lon, 4))
    y_key = lax.shift_right_arithmetic(own, 2) * 2 + far.astype(jnp.int32)
    turn = wide(mine, 16) & (wide(y_key, 16) == row16)
    acc = jnp.where(ids16 == 4, total(turn, (ids // 8 & 3) * 2 + near.astype(jnp.int32)), acc)
    meet[...] = acc.astype(jnp.int32)


def prep(base, south, north, west, east, light):
    flags, tab, meet = pl.pallas_call(
        prep_kernel,
        in_specs=[pl.BlockSpec(memory_space=VM)] * 6,
        out_specs=[pl.BlockSpec(memory_space=VM)] * 3,
        out_shape=[jax.ShapeDtypeStruct((128, 128), jnp.float32),
                   jax.ShapeDtypeStruct((8, 128), jnp.int32),
                   jax.ShapeDtypeStruct((16, 128), jnp.int32)],
        scratch_shapes=[VM((48, 128), jnp.float32)],
        cost_estimate=pl.CostEstimate(flops=10**7, bytes_accessed=10**5, transcendentals=0),
        name="prep",
    )(base, south, north, west, east, light)
    return flags.reshape(SIDE, 8, 128), tab, meet


def shift(x, axis, by):
    n = lax.axis_size(axis)
    return lax.ppermute(x, axis, [(i, (i + by) % n) for i in range(n)])


def swap(x):
    return lax.all_to_all(x, "lon", split_axis=0, concat_axis=0, tiled=True)


def on_device(tracers, phys_fine, mix_coarse, surf_light, land_mask, owner_map):
    wet = land_mask.astype(jnp.float32)
    base = jnp.concatenate([wet, owner_map.astype(jnp.float32)], axis=0)
    flags, tab, meet = prep(base, shift(base, "lat", 1), shift(base, "lat", -1),
                            shift(base, "lon", 1), shift(base, "lon", -1), surf_light)
    y, col = coarse(jnp.swapaxes(phys_fine, 1, 2), jnp.swapaxes(mix_coarse, 1, 2), flags)
    tab, y, col = lax.optimization_barrier((tab, y, col))
    west_col = shift(col, "lon", 1)
    south_row = shift(y[SIDE - 1, 48:96], "lat", 1)
    rows_out, w_out, e_out = pack(tab, tracers)
    came_west = shift(e_out, "lon", 1)
    came_east = shift(w_out, "lon", -1)
    y, rows_out = lax.optimization_barrier((y, rows_out))
    packed = package(tab, y, west_col, south_row)
    rows, phys = halo(True, meet, rows_out, packed)
    phys = phys.reshape(8, PHYS, CELLS)
    current, rows_out, w_out, e_out = step(False, tab, tracers, phys, rows, came_west, came_east)
    rows, came_west, came_east = halo(False, meet, rows_out, w_out, e_out)
    current, light_part = step(True, tab, current, phys, rows, came_west, came_east)
    return current, heat(tab, swap(light_part), wet, surf_light)


def solution(mesh):
    in_specs = (
        P(("lat", "lon"), None, None),
        P("lat", "lon", None),
        P("lat", "lon", None),
        P("lat", "lon"),
        P("lat", "lon"),
        P("lat", None),
    )
    out_specs = (P(("lat", "lon"), None, None), P(None, "lat", "lon"))
    return jax.shard_map(
        on_device, mesh=mesh, in_specs=in_specs, out_specs=out_specs, check_vma=False
    )
```

profile of v0, /device:TPU:2, one launch (start us, length us, event | category | flops | bytes accessed | tf_op | source)
XLA Modules:
  0.0 266.4 jit_solution(1829444931963269479)
XLA Ops:
  0.6 0.7 convert_element_type.7
  1.3 0.7 convert_element_type.6.wet
  2.0 6.6 %collective-permute-start.3 = (f32[17,128]{1,0:T(8,128)S(1)}, f32[17,128]{1,0:T(8,128)S(1)}, u32[]{:S(2)}, u32[]{:S(2)}) collective-permute-start(f32[17,128]{1,0:T(8,128)S(1)} %pad_maximum_fusion.base), channel_id=1, source_target_pairs={{0,15},{1,0},{2,1},{3,2},{4,3},{5,4},{6,5},{7,6},{8,7},{9,8},{10,9... | collective-permute-start | bytes 26120 | tf_op jit(solution)/shard_map/ppermute | solution.py:885
  8.6 0.5 collective-permute-start
  9.1 0.9 collective-permute-done.3.east
  10.0 5.6 %collective-permute-done.2.west = f32[17,128]{1,0:T(8,128)S(1)} collective-permute-done((f32[17,128]{1,0:T(8,128)S(1)}, f32[17,128]{1,0:T(8,128)S(1)}, u32[]{:S(2)}, u32[]{:S(2)}) %collective-permute-start.2) | collective-permute-done | bytes 8736 | tf_op jit(solution)/shard_map/ppermute | solution.py:885
  15.6 0.6 copy-done.7
  16.2 0.6 copy-done.9
  16.8 1.9 prep.1
  18.7 7.4 %coarse.1 = (f32[16,200,128]{2,1,0:T(8,128)}, f32[48,128]{1,0:T(8,128)}) custom-call(bf16[48,144,384]{2,1,0:T(8,128)(2,1)} %bitcast.14, bf16[16,48,128]{2,1,0:T(8,128)(2,1)} %bitcast.19, f32[16,8,128]{2,1,0:T(8,128)} %bitcast.20), custom_call_target="tpu_custom_call" | custom-call | flops 1000000000 | bytes 8000000 | tf_op jit(solution)/shard_map/coarse/pallas_call | solution.py:456
  26.0 8.8 %pack.1 = (f32[8,2,2,72,128]{4,3,2,1,0:T(8,128)}, f32[4,144,256]{2,1,0:T(8,128)}, f32[4,144,256]{2,1,0:T(8,128)}) custom-call(s32[8,128]{1,0:T(8,128)} %get-tuple-element.30.tab, f32[8,1152,256]{2,1,0:T(8,128)} %c_ref.3), custom_call_target="tpu_custom_call" | custom-call | flops 10000000 | bytes 12000000 | tf_op jit(solution)/shard_map/pack/pallas_call | solution.py:117
  34.8 5.3 %collective-permute-start.7 = (f32[4,144,256]{2,1,0:T(8,128)}, f32[4,144,256]{2,1,0:T(8,128)S(1)}, u32[]{:S(2)}, u32[]{:S(2)}) collective-permute-start(f32[4,144,256]{2,1,0:T(8,128)} %get-tuple-element.40), channel_id=1, source_target_pairs={{0,15},{1,0},{2,1},{3,2},{4,3},{5,4},{6,5},{7,6},{8,7},{9,8},{10,9... | collective-permute-start | bytes 1769480 | tf_op jit(solution)/shard_map/ppermute | solution.py:885
  40.1 0.7 slice_bitcast_fusion
  40.9 3.2 %collective-permute-done.5.row_ref = f32[48,128]{1,0:T(8,128)S(1)} collective-permute-done((f32[48,128]{1,0:T(8,128)S(1)}, f32[48,128]{1,0:T(8,128)S(1)}, u32[]{:S(2)}, u32[]{:S(2)}) %collective-permute-start.5) | collective-permute-done | bytes 24608 | tf_op jit(solution)/shard_map/ppermute | solution.py:885
  44.1 8.4 %collective-permute-done.4.col_ref = f32[48,128]{1,0:T(8,128)S(1)} collective-permute-done((f32[48,128]{1,0:T(8,128)S(1)}, f32[48,128]{1,0:T(8,128)S(1)}, u32[]{:S(2)}, u32[]{:S(2)}) %collective-permute-start.4) | collective-permute-done | bytes 24608 | tf_op jit(solution)/shard_map/ppermute | solution.py:885
  52.5 0.6 copy-done.5
  53.1 9.6 %package.1 = f32[8,224,256]{2,1,0:T(8,128)} custom-call(s32[8,128]{1,0:T(8,128)} %get-tuple-element.30.tab, f32[16,200,128]{2,1,0:T(8,128)} %get-tuple-element.35.y_ref, f32[48,128]{1,0:T(8,128)} %copy-done.5, f32[48,128]{1,0:T(8,128)} %copy-done.4), custom_call_target="tpu_custom_call" | custom-call | flops 10000000 | bytes 4000000 | tf_op jit(solution)/shard_map/package/pallas_call | solution.py:514
  62.7 62.5 %halo_phys.1 = (f32[16,2,72,128]{3,2,1,0:T(8,128)}, f32[4,2,224,256]{3,2,1,0:T(8,128)}) custom-call(s32[16,128]{1,0:T(8,128)} %get-tuple-element.31.refs_0_, f32[16,2,72,128]{3,2,1,0:T(8,128)} %bitcast.18, f32[4,2,224,256]{3,2,1,0:T(8,128)} %bitcast.13), custom_call_target="tpu_custom_call" | custom-call | flops 1000000 | bytes 100000000 | tf_op jit(solution)/shard_map/halo_phys/pallas_call | solution.py:710
  125.3 0.8 copy-done
  126.2 35.2 %first_step.1 = (f32[8,1152,256]{2,1,0:T(8,128)}, f32[8,2,2,72,128]{4,3,2,1,0:T(8,128)}, f32[4,144,256]{2,1,0:T(8,128)}, f32[4,144,256]{2,1,0:T(8,128)}) custom-call(s32[8,128]{1,0:T(8,128)} %get-tuple-element.30.tab, f32[8,1152,256]{2,1,0:T(8,128)} %c_ref.3, f32[8,224,256]{2,1,0:T(8,128)} %bitcast.11, f32[8,2,2,72,128]{4,3,2,1,0:T(8,128)} %bitcast.15, ...), custom_call_target="tpu_custom_call" | custom-call | flops 100000000 | bytes 25000000 | tf_op jit(solution)/shard_map/first_step/pallas_call | solution.py:393
  161.4 48.5 %halo.1 = (f32[16,2,72,128]{3,2,1,0:T(8,128)}, f32[4,144,256]{2,1,0:T(8,128)}, f32[4,144,256]{2,1,0:T(8,128)}) custom-call(s32[16,128]{1,0:T(8,128)} %get-tuple-element.31.refs_0_, f32[16,2,72,128]{3,2,1,0:T(8,128)} %bitcast.17, f32[4,144,256]{2,1,0:T(8,128)} %get-tuple-element.43.refs_2_, f32[4,144,256]{2,1,0:T(8,128)} %get-tuple-element.44.refs_3_), custom_call_target="tpu_custom_call" | custom-call | flops 1000000 | bytes 100000000 | tf_op jit(solution)/shard_map/halo/pallas_call | solution.py:710
  209.9 31.7 %last_step.1 = (f32[8,1152,256]{2,1,0:T(8,128)}, f32[16,48,256]{2,1,0:T(8,128)}) custom-call(s32[8,128]{1,0:T(8,128)} %get-tuple-element.30.tab, f32[8,1152,256]{2,1,0:T(8,128)} %get-tuple-element.41.c_ref, f32[8,224,256]{2,1,0:T(8,128)} %bitcast.12, f32[8,2,2,72,128]{4,3,2,1,0:T(8,128)} %bitcast.16, f32[4,144,256]{2,1,0:T(8,128)} %get-tuple-element.46.west, ...), custom_call_target="tpu_custom_call" | custom-call | flops 100000000 | bytes 25000000 | tf_op jit(solution)/shard_map/last_step/pallas_call | solution.py:393
  241.5 19.6 %all_to_all.5.got = f32[16,48,256]{2,1,0:T(8,128)} all-to-all(f32[16,48,256]{2,1,0:T(8,128)} %get-tuple-element.49), channel_id=1, replica_groups=mesh['lat'=8,'lon'=16] {'lon'}, dimensions={0} | all-to-all | bytes 1572864 | tf_op jit(solution)/shard_map/all_to_all | solution.py:889
  261.2 5.2 %heat.1 = bf16[48,48,384]{2,1,0:T(8,128)(2,1)} custom-call(s32[8,128]{1,0:T(8,128)} %get-tuple-element.30.tab, f32[16,48,256]{2,1,0:T(8,128)} %all_to_all.5.got, f32[16,128]{1,0:T(8,128)} %copy-done.3, f32[48,384]{1,0:T(8,128)} %light.3), custom_call_target="tpu_custom_call" | custom-call | flops 1000000000 | bytes 3000000 | tf_op jit(solution)/shard_map/heat/pallas_call | solution.py:753
  (28 shorter events, 0.3 us)
Async XLA Ops:
  2.0 24.1 %copy-start.3 = (f32[16,128]{1,0:T(8,128)}, f32[16,128]{1,0:T(8,128)S(1)}, u32[]{:S(2)}) copy-start(f32[16,128]{1,0:T(8,128)S(1)} %convert_element_type.6.wet) | copy-start | bytes 24580
  2.0 13.6 %copy-start.2 = (f32[17,128]{1,0:T(8,128)}, f32[17,128]{1,0:T(8,128)S(1)}, u32[]{:S(2)}) copy-start(f32[17,128]{1,0:T(8,128)S(1)} %pad_maximum_fusion.base) | copy-start | bytes 26116
  2.0 8.0 %collective-permute-start.3 = (f32[17,128]{1,0:T(8,128)S(1)}, f32[17,128]{1,0:T(8,128)S(1)}, u32[]{:S(2)}, u32[]{:S(2)}) collective-permute-start(f32[17,128]{1,0:T(8,128)S(1)} %pad_maximum_fusion.base), channel_id=1, source_target_pairs={{0,15},{1,0},{2,1},{3,2},{4,3},{5,4},{6,5},{7,6},{8,7},{9,8},{10,9... | collective-permute-start | bytes 26120 | tf_op jit(solution)/shard_map/ppermute | solution.py:885
  8.6 7.0 %collective-permute-start.2 = (f32[17,128]{1,0:T(8,128)S(1)}, f32[17,128]{1,0:T(8,128)S(1)}, u32[]{:S(2)}, u32[]{:S(2)}) collective-permute-start(f32[17,128]{1,0:T(8,128)S(1)} %pad_maximum_fusion.base), channel_id=1, source_target_pairs={{0,1},{1,2},{2,3},{3,4},{4,5},{5,6},{6,7},{7,8},{8,9},{9,10},{10,1... | collective-permute-start | bytes 26120 | tf_op jit(solution)/shard_map/ppermute | solution.py:885
  8.6 7.0 %collective-permute-start.1 = (f32[17,128]{1,0:T(8,128)S(1)}, f32[17,128]{1,0:T(8,128)S(1)}, u32[]{:S(2)}, u32[]{:S(2)}) collective-permute-start(f32[17,128]{1,0:T(8,128)S(1)} %pad_maximum_fusion.base), channel_id=1, source_target_pairs={{0,112},{16,0},{32,16},{48,32},{64,48},{80,64},{96,80},{112,96},{1... | collective-permute-start | bytes 26120 | tf_op jit(solution)/shard_map/ppermute | solution.py:885
  8.6 7.0 %collective-permute-start = (f32[17,128]{1,0:T(8,128)S(1)}, f32[17,128]{1,0:T(8,128)S(1)}, u32[]{:S(2)}, u32[]{:S(2)}) collective-permute-start(f32[17,128]{1,0:T(8,128)S(1)} %pad_maximum_fusion.base), channel_id=1, source_target_pairs={{0,16},{16,32},{32,48},{48,64},{64,80},{80,96},{96,112},{112,0},{1... | collective-permute-start | bytes 26120 | tf_op jit(solution)/shard_map/ppermute | solution.py:885
  10.0 5.6 %copy-start.6 = (f32[17,128]{1,0:T(8,128)}, f32[17,128]{1,0:T(8,128)S(1)}, u32[]{:S(2)}) copy-start(f32[17,128]{1,0:T(8,128)S(1)} %collective-permute-done.3.east) | copy-start | bytes 26116
  15.6 0.6 copy-start.7
  15.6 0.6 copy-start.8
  16.2 0.6 copy-start.9
  26.0 14.8 %copy-start.10 = (f32[48,128]{1,0:T(8,128)S(1)}, f32[48,128]{1,0:T(8,128)}, u32[]{:S(2)}) copy-start(f32[48,128]{1,0:T(8,128)} %get-tuple-element.36) | copy-start | bytes 73732
  34.8 90.4 %collective-permute-start.6 = (f32[4,144,256]{2,1,0:T(8,128)}, f32[4,144,256]{2,1,0:T(8,128)S(1)}, u32[]{:S(2)}, u32[]{:S(2)}) collective-permute-start(f32[4,144,256]{2,1,0:T(8,128)} %get-tuple-element.39), channel_id=1, source_target_pairs={{0,1},{1,2},{2,3},{3,4},{4,5},{5,6},{6,7},{7,8},{8,9},{9,10},{10,1... | collective-permute-start | bytes 1769480 | tf_op jit(solution)/shard_map/ppermute | solution.py:885
  34.8 90.4 %collective-permute-start.7 = (f32[4,144,256]{2,1,0:T(8,128)}, f32[4,144,256]{2,1,0:T(8,128)S(1)}, u32[]{:S(2)}, u32[]{:S(2)}) collective-permute-start(f32[4,144,256]{2,1,0:T(8,128)} %get-tuple-element.40), channel_id=1, source_target_pairs={{0,15},{1,0},{2,1},{3,2},{4,3},{5,4},{6,5},{7,6},{8,7},{9,8},{10,9... | collective-permute-start | bytes 1769480 | tf_op jit(solution)/shard_map/ppermute | solution.py:885
  40.9 3.3 %collective-permute-start.5 = (f32[48,128]{1,0:T(8,128)S(1)}, f32[48,128]{1,0:T(8,128)S(1)}, u32[]{:S(2)}, u32[]{:S(2)}) collective-permute-start(f32[48,128]{1,0:T(8,128)S(1)} %slice_bitcast_fusion), channel_id=1, source_target_pairs={{0,16},{16,32},{32,48},{48,64},{64,80},{80,96},{96,112},{112,0},{1... | collective-permute-start | bytes 73736 | tf_op jit(solution)/shard_map/ppermute | solution.py:885
  40.9 11.6 %collective-permute-start.4 = (f32[48,128]{1,0:T(8,128)S(1)}, f32[48,128]{1,0:T(8,128)S(1)}, u32[]{:S(2)}, u32[]{:S(2)}) collective-permute-start(f32[48,128]{1,0:T(8,128)S(1)} %copy-done.10), channel_id=1, source_target_pairs={{0,1},{1,2},{2,3},{3,4},{4,5},{5,6},{6,7},{7,8},{8,9},{9,10},{10,1... | collective-permute-start | bytes 73736 | tf_op jit(solution)/shard_map/ppermute | solution.py:885
  44.1 8.4 %copy-start.4 = (f32[48,128]{1,0:T(8,128)}, f32[48,128]{1,0:T(8,128)S(1)}, u32[]{:S(2)}) copy-start(f32[48,128]{1,0:T(8,128)S(1)} %collective-permute-done.5.row_ref) | copy-start | bytes 73732
  52.5 0.6 copy-start.5
  125.2 0.8 copy-start
  125.3 1.0 copy-start.1
where the time goes:
time: 269 us; the launch traced here: 266 us
  Pallas kernels  211 us (78%)
  blocking collectives  19.6 us (7%)
  waiting for transfers between devices  18.1 us (7%)
  starting transfers between devices  12.4 us (5%)
  local copies, waits for them, and re-layouts  3.52 us (1%)
    pallas_call x2, Pallas kernels, halo(): pl.pallas_call(functools.partial(halo_kernel, first), in_specs=[pl.BlockS...  111 us
    pallas_call x2, Pallas kernels, step(): pl.pallas_call(last_kernel if last else first_kernel, grid_spec=pltpu.Pre...  66.8 us
    all_to_all x1, blocking collectives, swap(): return lax.all_to_all(x, 'lon', split_axis=0, concat_axis=0, tiled=True)  19.6 us
    ppermute x8, waiting for transfers between devices, shift(): return lax.ppermute(x, axis, [(i, (i + by) % n) for i in range(n)])  18.1 us
    ppermute x8, starting transfers between devices, shift(): return lax.ppermute(x, axis, [(i, (i + by) % n) for i in range(n)])  12.4 us
    pallas_call x1, Pallas kernels, package(): pl.pallas_call(package_kernel, in_specs=[pl.BlockSpec(memory_space=pltpu....  9.58 us
    pallas_call x1, Pallas kernels, pack(): pl.pallas_call(pack_kernel, grid_spec=pltpu.PrefetchScalarGridSpec(num_sc...  8.75 us
    pallas_call x1, Pallas kernels, coarse(): pl.pallas_call(coarse_kernel, grid=(SIDE // 2,), in_specs=[pl.BlockSpec((...  7.35 us
  transfers between devices with their start and end apart: 8, of which 4 were waited for; matrix products, arithmetic and copies ran while one was open for 0% of the time, Pallas kernels for 27%

commit v1 on v0

--- a/solution.py
+++ b/solution.py
@@ -545,11 +545,11 @@
 def halo_kernel(first, *refs):
     if first:
         (tab, up_ref, phys, rows_ref, phys_out, got_s, got_n, pick, turn, mid0, mid1, mid2, mid3,
-         up_send, up_recv, dn_send, dn_recv, z_send, z_recv, y_send, y_recv, own) = refs
+         up_send, up_recv, dn_send, dn_recv, z_send, z_recv, y_send, y_recv, own, rest, home) = refs
         mid = (mid0, mid1, mid2, mid3)
     else:
         (tab, up_ref, w_ref, e_ref, rows_ref, from_w, from_e, got_s, got_n, pick,
-         up_send, up_recv, dn_send, dn_recv, we_send, we_recv) = refs
+         up_send, up_recv, dn_send, dn_recv, we_send, we_recv, home) = refs
     lat, lon = lax.axis_index("lat"), lax.axis_index("lon")
     bands, count = lax.axis_size("lat"), lax.axis_size("lon")
     sides = (lax.rem(lat + 1, bands), lax.rem(lat + bands - 1, bands))
@@ -608,6 +608,12 @@
         y = lax.rem(row + 4 - d, 4)
         return remote(turn.at[y, :, piece(p)], phys_out.at[y, :, piece(p)], y_send.at[p, d], y_recv.at[p, d], (lat, 4 * y + place))
 
+    def at_home(n):
+        return pltpu.make_async_copy(pick.at[n, lon], rows_ref.at[lon, n], home.at[n])
+
+    def remain(p):
+        return pltpu.make_async_copy(turn.at[row, :, piece(p)], phys_out.at[row, :, piece(p)], rest.at[p])
+
     def lift(n):
         for d in ORDER:
             up(n, d).start()
@@ -621,7 +627,8 @@
             pick[n, o] = jnp.where(tab[o, 2 * n + 1] > 0, value, 0.0)
 
         each(0, count, choose)
-        rows_ref[lon, n] = pick[n, lon]
+        keep = at_home(n)
+        keep.start()
         for d in ORDER[1:]:
             down(n, d).start()
 
@@ -644,7 +651,7 @@
         each(0, 8, sort)
         for d in (2, 1, 3):
             by_y(p, d).start()
-        phys_out[row, :, piece(p)] = turn[row, :, piece(p)]
+        remain(p).start()
 
     if first:
         send_z(0)
@@ -669,6 +676,7 @@
         to_w.start()
         descend(1)
     for n in range(2):
+        at_home(n).wait()
         for d in ORDER[1:]:
             down_from(n, d).wait_recv()
     for n in range(2):
@@ -682,6 +690,7 @@
                 from_y(p, d).wait_recv()
                 by_z(p, d).wait_send()
                 by_y(p, d).wait_send()
+            remain(p).wait()
     else:
         to_e.wait()
         to_w.wait()
@@ -689,7 +698,6 @@
 
 def halo(first, tab, rows, *rest):
     anywhere = pl.BlockSpec(memory_space=pl.ANY)
-    here = pl.BlockSpec(memory_space=VM)
     edge = jax.ShapeDtypeStruct((4, ROWS3, CELLS), jnp.float32)
     dma = pltpu.SemaphoreType.DMA
     sent = pltpu.VMEM((4, 2, PHYS, CELLS), jnp.float32)
@@ -698,18 +706,18 @@
                VM((2, 16, HALF, 128), jnp.float32)]
     sems = [dma((2, 16)), dma((2, 16)), dma((2, 16)), dma((2, 16))]
     if first:
-        in_specs, out_specs = [here], [here, here]
+        in_specs, out_specs = [anywhere], [anywhere, anywhere]
         out.append(jax.ShapeDtypeStruct((4, 2, PHYS, CELLS), jnp.float32))
         scratch += [sent] + [VM((4, 2, PART, CELLS), jnp.float32)] * PARTS
-        scratch += sems + [dma((PARTS, 4))] * 4 + [dma((PARTS,))]
+        scratch += sems + [dma((PARTS, 4))] * 4 + [dma((PARTS,)), dma((PARTS,)), dma((2,))]
         rest = [rest[0].reshape(4, 2, PHYS, CELLS)]
     else:
-        in_specs, out_specs = [anywhere] * 2, [here] + [anywhere] * 2
+        in_specs, out_specs = [anywhere] * 2, [anywhere] * 3
         out += [edge, edge]
-        scratch += sems + [dma((2,)), dma((2,))]
+        scratch += sems + [dma((2,)), dma((2,)), dma((2,))]
     rows, *more = pl.pallas_call(
         functools.partial(halo_kernel, first),
-        in_specs=[pl.BlockSpec(memory_space=pltpu.SMEM), here] + in_specs,
+        in_specs=[pl.BlockSpec(memory_space=pltpu.SMEM), anywhere] + in_specs,
         out_specs=out_specs,
         out_shape=out,
         scratch_shapes=scratch,

time: 269 us -> 265 us (0.985)
  Pallas kernels: 211 us -> 207 us
    pallas_call x2, Pallas kernels: 111 us -> 107 us  [halo(): pl.pallas_call(functools.partial(halo_kernel, first), in_specs=[pl.BlockS...]
where the time goes in v1:
time: 265 us; the launch traced here: 263 us
  Pallas kernels  207 us (78%)
  blocking collectives  19.6 us (7%)
  waiting for transfers between devices  18.1 us (7%)
  starting transfers between devices  12.4 us (5%)
  local copies, waits for them, and re-layouts  3.52 us (1%)
    pallas_call x2, Pallas kernels, halo(): pl.pallas_call(functools.partial(halo_kernel, first), in_specs=[pl.BlockS...  107 us
    pallas_call x2, Pallas kernels, step(): pl.pallas_call(last_kernel if last else first_kernel, grid_spec=pltpu.Pre...  66.8 us
    all_to_all x1, blocking collectives, swap(): return lax.all_to_all(x, 'lon', split_axis=0, concat_axis=0, tiled=True)  19.6 us
    ppermute x8, waiting for transfers between devices, shift(): return lax.ppermute(x, axis, [(i, (i + by) % n) for i in range(n)])  18.1 us
    ppermute x8, starting transfers between devices, shift(): return lax.ppermute(x, axis, [(i, (i + by) % n) for i in range(n)])  12.4 us
    pallas_call x1, Pallas kernels, package(): pl.pallas_call(package_kernel, in_specs=[pl.BlockSpec(memory_space=pltpu....  9.58 us
    pallas_call x1, Pallas kernels, pack(): pl.pallas_call(pack_kernel, grid_spec=pltpu.PrefetchScalarGridSpec(num_sc...  8.75 us
    pallas_call x1, Pallas kernels, coarse(): pl.pallas_call(coarse_kernel, grid=(SIDE // 2,), in_specs=[pl.BlockSpec((...  7.35 us
  transfers between devices with their start and end apart: 8, of which 4 were waited for; matrix products, arithmetic and copies ran while one was open for 0% of the time, Pallas kernels for 27%

profile of v1, /device:TPU:2, one launch (start us, length us, event | category | flops | bytes accessed | tf_op | source)
XLA Modules:
  0.0 262.9 jit_solution(14655016699006206920)
XLA Ops:
  0.6 0.7 convert_element_type.7
  1.3 0.7 convert_element_type.6.wet
  2.0 6.6 %collective-permute-start.3 = (f32[17,128]{1,0:T(8,128)S(1)}, f32[17,128]{1,0:T(8,128)S(1)}, u32[]{:S(2)}, u32[]{:S(2)}) collective-permute-start(f32[17,128]{1,0:T(8,128)S(1)} %pad_maximum_fusion.base), channel_id=1, source_target_pairs={{0,15},{1,0},{2,1},{3,2},{4,3},{5,4},{6,5},{7,6},{8,7},{9,8},{10,9... | collective-permute-start | bytes 26120 | tf_op jit(solution)/shard_map/ppermute | solution.py:893
  8.6 0.5 collective-permute-start
  9.1 0.9 collective-permute-done.3.east
  10.0 5.6 %collective-permute-done.2.west = f32[17,128]{1,0:T(8,128)S(1)} collective-permute-done((f32[17,128]{1,0:T(8,128)S(1)}, f32[17,128]{1,0:T(8,128)S(1)}, u32[]{:S(2)}, u32[]{:S(2)}) %collective-permute-start.2) | collective-permute-done | bytes 8736 | tf_op jit(solution)/shard_map/ppermute | solution.py:893
  15.6 0.6 copy-done.7
  16.2 0.6 copy-done.9
  16.8 1.9 prep.1
  18.7 7.4 %coarse.1 = (f32[16,200,128]{2,1,0:T(8,128)}, f32[48,128]{1,0:T(8,128)}) custom-call(bf16[48,144,384]{2,1,0:T(8,128)(2,1)} %bitcast.14, bf16[16,48,128]{2,1,0:T(8,128)(2,1)} %bitcast.19, f32[16,8,128]{2,1,0:T(8,128)} %bitcast.20), custom_call_target="tpu_custom_call" | custom-call | flops 1000000000 | bytes 8000000 | tf_op jit(solution)/shard_map/coarse/pallas_call | solution.py:456
  26.0 8.8 %pack.1 = (f32[8,2,2,72,128]{4,3,2,1,0:T(8,128)}, f32[4,144,256]{2,1,0:T(8,128)}, f32[4,144,256]{2,1,0:T(8,128)}) custom-call(s32[8,128]{1,0:T(8,128)} %get-tuple-element.30.tab, f32[8,1152,256]{2,1,0:T(8,128)} %c_ref.3), custom_call_target="tpu_custom_call" | custom-call | flops 10000000 | bytes 12000000 | tf_op jit(solution)/shard_map/pack/pallas_call | solution.py:117
  34.8 5.3 %collective-permute-start.7 = (f32[4,144,256]{2,1,0:T(8,128)}, f32[4,144,256]{2,1,0:T(8,128)S(1)}, u32[]{:S(2)}, u32[]{:S(2)}) collective-permute-start(f32[4,144,256]{2,1,0:T(8,128)} %get-tuple-element.40), channel_id=1, source_target_pairs={{0,15},{1,0},{2,1},{3,2},{4,3},{5,4},{6,5},{7,6},{8,7},{9,8},{10,9... | collective-permute-start | bytes 1769480 | tf_op jit(solution)/shard_map/ppermute | solution.py:893
  40.1 0.7 slice_bitcast_fusion
  40.9 3.2 %collective-permute-done.5.row_ref = f32[48,128]{1,0:T(8,128)S(1)} collective-permute-done((f32[48,128]{1,0:T(8,128)S(1)}, f32[48,128]{1,0:T(8,128)S(1)}, u32[]{:S(2)}, u32[]{:S(2)}) %collective-permute-start.5) | collective-permute-done | bytes 24608 | tf_op jit(solution)/shard_map/ppermute | solution.py:893
  44.1 8.4 %collective-permute-done.4.col_ref = f32[48,128]{1,0:T(8,128)S(1)} collective-permute-done((f32[48,128]{1,0:T(8,128)S(1)}, f32[48,128]{1,0:T(8,128)S(1)}, u32[]{:S(2)}, u32[]{:S(2)}) %collective-permute-start.4) | collective-permute-done | bytes 24608 | tf_op jit(solution)/shard_map/ppermute | solution.py:893
  52.5 0.6 copy-done.5
  53.1 9.6 %package.1 = f32[8,224,256]{2,1,0:T(8,128)} custom-call(s32[8,128]{1,0:T(8,128)} %get-tuple-element.30.tab, f32[16,200,128]{2,1,0:T(8,128)} %get-tuple-element.35.y_ref, f32[48,128]{1,0:T(8,128)} %copy-done.5, f32[48,128]{1,0:T(8,128)} %copy-done.4), custom_call_target="tpu_custom_call" | custom-call | flops 10000000 | bytes 4000000 | tf_op jit(solution)/shard_map/package/pallas_call | solution.py:514
  62.7 60.2 %halo_phys.1 = (f32[16,2,72,128]{3,2,1,0:T(8,128)}, f32[4,2,224,256]{3,2,1,0:T(8,128)}) custom-call(s32[16,128]{1,0:T(8,128)} %get-tuple-element.31.refs_0_, f32[16,2,72,128]{3,2,1,0:T(8,128)} %bitcast.18, f32[4,2,224,256]{3,2,1,0:T(8,128)} %bitcast.13), custom_call_target="tpu_custom_call" | custom-call | flops 1000000 | bytes 100000000 | tf_op jit(solution)/shard_map/halo_phys/pallas_call | solution.py:718
  123.0 0.8 copy-done
  123.9 35.2 %first_step.1 = (f32[8,1152,256]{2,1,0:T(8,128)}, f32[8,2,2,72,128]{4,3,2,1,0:T(8,128)}, f32[4,144,256]{2,1,0:T(8,128)}, f32[4,144,256]{2,1,0:T(8,128)}) custom-call(s32[8,128]{1,0:T(8,128)} %get-tuple-element.30.tab, f32[8,1152,256]{2,1,0:T(8,128)} %c_ref.3, f32[8,224,256]{2,1,0:T(8,128)} %bitcast.11, f32[8,2,2,72,128]{4,3,2,1,0:T(8,128)} %bitcast.15, ...), custom_call_target="tpu_custom_call" | custom-call | flops 100000000 | bytes 25000000 | tf_op jit(solution)/shard_map/first_step/pallas_call | solution.py:393
  159.1 47.3 %halo.1 = (f32[16,2,72,128]{3,2,1,0:T(8,128)}, f32[4,144,256]{2,1,0:T(8,128)}, f32[4,144,256]{2,1,0:T(8,128)}) custom-call(s32[16,128]{1,0:T(8,128)} %get-tuple-element.31.refs_0_, f32[16,2,72,128]{3,2,1,0:T(8,128)} %bitcast.17, f32[4,144,256]{2,1,0:T(8,128)} %get-tuple-element.43.refs_2_, f32[4,144,256]{2,1,0:T(8,128)} %get-tuple-element.44.refs_3_), custom_call_target="tpu_custom_call" | custom-call | flops 1000000 | bytes 100000000 | tf_op jit(solution)/shard_map/halo/pallas_call | solution.py:718
  206.4 31.7 %last_step.1 = (f32[8,1152,256]{2,1,0:T(8,128)}, f32[16,48,256]{2,1,0:T(8,128)}) custom-call(s32[8,128]{1,0:T(8,128)} %get-tuple-element.30.tab, f32[8,1152,256]{2,1,0:T(8,128)} %get-tuple-element.41.c_ref, f32[8,224,256]{2,1,0:T(8,128)} %bitcast.12, f32[8,2,2,72,128]{4,3,2,1,0:T(8,128)} %bitcast.16, f32[4,144,256]{2,1,0:T(8,128)} %get-tuple-element.46.west, ...), custom_call_target="tpu_custom_call" | custom-call | flops 100000000 | bytes 25000000 | tf_op jit(solution)/shard_map/last_step/pallas_call | solution.py:393
  238.0 19.6 %all_to_all.5.got = f32[16,48,256]{2,1,0:T(8,128)} all-to-all(f32[16,48,256]{2,1,0:T(8,128)} %get-tuple-element.49), channel_id=1, replica_groups=mesh['lat'=8,'lon'=16] {'lon'}, dimensions={0} | all-to-all | bytes 1572864 | tf_op jit(solution)/shard_map/all_to_all | solution.py:897
  257.7 5.2 %heat.1 = bf16[48,48,384]{2,1,0:T(8,128)(2,1)} custom-call(s32[8,128]{1,0:T(8,128)} %get-tuple-element.30.tab, f32[16,48,256]{2,1,0:T(8,128)} %all_to_all.5.got, f32[16,128]{1,0:T(8,128)} %copy-done.3, f32[48,384]{1,0:T(8,128)} %light.3), custom_call_target="tpu_custom_call" | custom-call | flops 1000000000 | bytes 3000000 | tf_op jit(solution)/shard_map/heat/pallas_call | solution.py:761
  (28 shorter events, 0.3 us)
Async XLA Ops:
  2.0 24.1 %copy-start.3 = (f32[16,128]{1,0:T(8,128)}, f32[16,128]{1,0:T(8,128)S(1)}, u32[]{:S(2)}) copy-start(f32[16,128]{1,0:T(8,128)S(1)} %convert_element_type.6.wet) | copy-start | bytes 24580
  2.0 13.6 %copy-start.2 = (f32[17,128]{1,0:T(8,128)}, f32[17,128]{1,0:T(8,128)S(1)}, u32[]{:S(2)}) copy-start(f32[17,128]{1,0:T(8,128)S(1)} %pad_maximum_fusion.base) | copy-start | bytes 26116
  2.0 8.0 %collective-permute-start.3 = (f32[17,128]{1,0:T(8,128)S(1)}, f32[17,128]{1,0:T(8,128)S(1)}, u32[]{:S(2)}, u32[]{:S(2)}) collective-permute-start(f32[17,128]{1,0:T(8,128)S(1)} %pad_maximum_fusion.base), channel_id=1, source_target_pairs={{0,15},{1,0},{2,1},{3,2},{4,3},{5,4},{6,5},{7,6},{8,7},{9,8},{10,9... | collective-permute-start | bytes 26120 | tf_op jit(solution)/shard_map/ppermute | solution.py:893
  8.6 7.0 %collective-permute-start.2 = (f32[17,128]{1,0:T(8,128)S(1)}, f32[17,128]{1,0:T(8,128)S(1)}, u32[]{:S(2)}, u32[]{:S(2)}) collective-permute-start(f32[17,128]{1,0:T(8,128)S(1)} %pad_maximum_fusion.base), channel_id=1, source_target_pairs={{0,1},{1,2},{2,3},{3,4},{4,5},{5,6},{6,7},{7,8},{8,9},{9,10},{10,1... | collective-permute-start | bytes 26120 | tf_op jit(solution)/shard_map/ppermute | solution.py:893
  8.6 7.0 %collective-permute-start.1 = (f32[17,128]{1,0:T(8,128)S(1)}, f32[17,128]{1,0:T(8,128)S(1)}, u32[]{:S(2)}, u32[]{:S(2)}) collective-permute-start(f32[17,128]{1,0:T(8,128)S(1)} %pad_maximum_fusion.base), channel_id=1, source_target_pairs={{0,112},{16,0},{32,16},{48,32},{64,48},{80,64},{96,80},{112,96},{1... | collective-permute-start | bytes 26120 | tf_op jit(solution)/shard_map/ppermute | solution.py:893
  8.6 7.0 %collective-permute-start = (f32[17,128]{1,0:T(8,128)S(1)}, f32[17,128]{1,0:T(8,128)S(1)}, u32[]{:S(2)}, u32[]{:S(2)}) collective-permute-start(f32[17,128]{1,0:T(8,128)S(1)} %pad_maximum_fusion.base), channel_id=1, source_target_pairs={{0,16},{16,32},{32,48},{48,64},{64,80},{80,96},{96,112},{112,0},{1... | collective-permute-start | bytes 26120 | tf_op jit(solution)/shard_map/ppermute | solution.py:893
  10.0 5.6 %copy-start.6 = (f32[17,128]{1,0:T(8,128)}, f32[17,128]{1,0:T(8,128)S(1)}, u32[]{:S(2)}) copy-start(f32[17,128]{1,0:T(8,128)S(1)} %collective-permute-done.3.east) | copy-start | bytes 26116
  15.6 0.6 copy-start.7
  15.6 0.6 copy-start.8
  16.2 0.6 copy-start.9
  26.0 14.8 %copy-start.10 = (f32[48,128]{1,0:T(8,128)S(1)}, f32[48,128]{1,0:T(8,128)}, u32[]{:S(2)}) copy-start(f32[48,128]{1,0:T(8,128)} %get-tuple-element.36) | copy-start | bytes 73732
  34.8 88.1 %collective-permute-start.6 = (f32[4,144,256]{2,1,0:T(8,128)}, f32[4,144,256]{2,1,0:T(8,128)S(1)}, u32[]{:S(2)}, u32[]{:S(2)}) collective-permute-start(f32[4,144,256]{2,1,0:T(8,128)} %get-tuple-element.39), channel_id=1, source_target_pairs={{0,1},{1,2},{2,3},{3,4},{4,5},{5,6},{6,7},{7,8},{8,9},{9,10},{10,1... | collective-permute-start | bytes 1769480 | tf_op jit(solution)/shard_map/ppermute | solution.py:893
  34.8 88.1 %collective-permute-start.7 = (f32[4,144,256]{2,1,0:T(8,128)}, f32[4,144,256]{2,1,0:T(8,128)S(1)}, u32[]{:S(2)}, u32[]{:S(2)}) collective-permute-start(f32[4,144,256]{2,1,0:T(8,128)} %get-tuple-element.40), channel_id=1, source_target_pairs={{0,15},{1,0},{2,1},{3,2},{4,3},{5,4},{6,5},{7,6},{8,7},{9,8},{10,9... | collective-permute-start | bytes 1769480 | tf_op jit(solution)/shard_map/ppermute | solution.py:893
  40.9 3.3 %collective-permute-start.5 = (f32[48,128]{1,0:T(8,128)S(1)}, f32[48,128]{1,0:T(8,128)S(1)}, u32[]{:S(2)}, u32[]{:S(2)}) collective-permute-start(f32[48,128]{1,0:T(8,128)S(1)} %slice_bitcast_fusion), channel_id=1, source_target_pairs={{0,16},{16,32},{32,48},{48,64},{64,80},{80,96},{96,112},{112,0},{1... | collective-permute-start | bytes 73736 | tf_op jit(solution)/shard_map/ppermute | solution.py:893
  40.9 11.6 %collective-permute-start.4 = (f32[48,128]{1,0:T(8,128)S(1)}, f32[48,128]{1,0:T(8,128)S(1)}, u32[]{:S(2)}, u32[]{:S(2)}) collective-permute-start(f32[48,128]{1,0:T(8,128)S(1)} %copy-done.10), channel_id=1, source_target_pairs={{0,1},{1,2},{2,3},{3,4},{4,5},{5,6},{6,7},{7,8},{8,9},{9,10},{10,1... | collective-permute-start | bytes 73736 | tf_op jit(solution)/shard_map/ppermute | solution.py:893
  44.1 8.4 %copy-start.4 = (f32[48,128]{1,0:T(8,128)}, f32[48,128]{1,0:T(8,128)S(1)}, u32[]{:S(2)}) copy-start(f32[48,128]{1,0:T(8,128)S(1)} %collective-permute-done.5.row_ref) | copy-start | bytes 73732
  52.5 0.6 copy-start.5
  122.9 0.8 copy-start
  123.0 1.0 copy-start.1

commit v2 on v1

--- a/solution.py
+++ b/solution.py
@@ -462,11 +462,11 @@
             pl.BlockSpec((2, 8, 128), lambda r: (r, 0, 0)),
         ],
         out_specs=[
-            pl.BlockSpec((2, 200, 128), lambda r: (r, 0, 0)),
+            pl.BlockSpec((2, PHYS, 128), lambda r: (r, 0, 0)),
             pl.BlockSpec((LEV, 128), lambda r: (0, 0)),
         ],
         out_shape=[
-            jax.ShapeDtypeStruct((SIDE, 200, 128), jnp.float32),
+            jax.ShapeDtypeStruct((SIDE, PHYS, 128), jnp.float32),
             jax.ShapeDtypeStruct((LEV, 128), jnp.float32),
         ],
         scratch_shapes=[VM((384, 128), jnp.bfloat16), VM((384, 128), jnp.bfloat16)],
@@ -475,12 +475,14 @@
     )(phys_t, mix_t, flags)
 
 
-def package_kernel(tab, y_ref, col_ref, row_ref, out):
+def package_kernel(tab, y_ref, col_ref, row_ref, out, faces):
+    step = pl.program_id(0)
     group = lax.broadcasted_iota(jnp.int32, (8, 128), 1) // SIDE
 
     def chunk(i, carry):
         at = pl.ds(pl.multiple_of(8 * i, 8), 8)
         for h in range(2):
+            hs = slice(128 * h, 128 * h + 128)
             vals = [y_ref[8 * h + g, at, :] for g in range(8)]
             for d in (1, 2, 4):
                 lower = (group // d) % 2 == 0
@@ -491,30 +493,47 @@
                     vals[g] = jnp.where(lower, a, roll(b, 16 * d))
                     vals[g + d] = jnp.where(lower, roll(a, 128 - 16 * d), b)
             for k in range(TILE):
-                out[tab[k, 7], at, 128 * h:128 * h + 128] = vals[k]
+                out[tab[k, 7], at, hs] = vals[k]
+
+            @pl.when(step < 2)
+            def _():
+                for k in range(TILE):
+                    faces[k, pl.ds(pl.multiple_of(32 * step + 8 * i, 8), 8), hs] = vals[k]
         return carry
 
-    lax.fori_loop(0, 25, chunk, 0)
-    i = lax.broadcasted_iota(jnp.int32, (256, 128), 0)
-    j = lax.broadcasted_iota(jnp.int32, (256, 128), 1)
-    last = (i == SIDE * j + SIDE - 1).astype(jnp.float32)
-    low = lanes() < SIDE
-    for k in range(TILE):
-        if k:
-            west = jnp.dot(out[tab[k - 1, 7], 0:48, :], last, precision=lax.Precision.HIGHEST,
-                           preferred_element_type=jnp.float32)
-        else:
-            west = col_ref[...]
-        edge = jnp.where(low, west, roll(row_ref[...], (16 - 16 * k) % 128))
-        out[tab[k, 7], 200:224, 0:128] = edge[0:24]
-        out[tab[k, 7], 200:224, 128:256] = edge[24:48]
+    lax.fori_loop(0, jnp.where(step == 6, 1, 4), chunk, 0)
+
+    @pl.when(step == 6)
+    def _():
+        i = lax.broadcasted_iota(jnp.int32, (256, 128), 0)
+        j = lax.broadcasted_iota(jnp.int32, (256, 128), 1)
+        last = (i == SIDE * j + SIDE - 1).astype(jnp.float32)
+        low = lanes() < SIDE
+        for k in range(TILE):
+            if k:
+                west = jnp.dot(faces[k - 1, 0:48, :], last, precision=lax.Precision.HIGHEST,
+                               preferred_element_type=jnp.float32)
+            else:
+                west = col_ref[...]
+            edge = jnp.where(low, west, roll(row_ref[...], (16 - 16 * k) % 128))
+            out[tab[k, 7], 8:32, 0:128] = edge[0:24]
+            out[tab[k, 7], 8:32, 128:256] = edge[24:48]
 
 
 def package(tab, y, col, row):
     return pl.pallas_call(
         package_kernel,
-        in_specs=[pl.BlockSpec(memory_space=pltpu.SMEM)] + [pl.BlockSpec(memory_space=VM)] * 3,
-        out_specs=pl.BlockSpec(memory_space=VM),
+        grid_spec=pltpu.PrefetchScalarGridSpec(
+            num_scalar_prefetch=1,
+            grid=(7,),
+            in_specs=[
+                pl.BlockSpec((SIDE, 32, 128), lambda i, tab: (0, i, 0)),
+                pl.BlockSpec((LEV, 128), lambda i, tab: (0, 0)),
+                pl.BlockSpec((LEV, 128), lambda i, tab: (0, 0)),
+            ],
+            out_specs=pl.BlockSpec((8, 32, CELLS), lambda i, tab: (0, i, 0)),
+            scratch_shapes=[VM((TILE, 64, CELLS), jnp.float32)],
+        ),
         out_shape=jax.ShapeDtypeStruct((8, PHYS, CELLS), jnp.float32),
         cost_estimate=pl.CostEstimate(flops=10**7, bytes_accessed=4 * 10**6, transcendentals=0),
         name="package",
@@ -529,7 +548,7 @@
                                         device_id=where, device_id_type=MESH)
 
 
-PARTS = 4
+PARTS = 7
 PART = PHYS // PARTS
 ORDER = (0, 5, 10, 15, 4, 1, 8, 2, 12, 3, 6, 9, 7, 13, 11, 14)
 
@@ -544,9 +563,9 @@
 
 def halo_kernel(first, *refs):
     if first:
-        (tab, up_ref, phys, rows_ref, phys_out, got_s, got_n, pick, turn, mid0, mid1, mid2, mid3,
-         up_send, up_recv, dn_send, dn_recv, z_send, z_recv, y_send, y_recv, own, rest, home) = refs
-        mid = (mid0, mid1, mid2, mid3)
+        tab, up_ref, phys, rows_ref, phys_out, got_s, got_n, pick, turn = refs[:9]
+        mid = refs[9:9 + PARTS]
+        (up_send, up_recv, dn_send, dn_recv, z_send, z_recv, y_send, y_recv, own, rest, home) = refs[9 + PARTS:]
     else:
         (tab, up_ref, w_ref, e_ref, rows_ref, from_w, from_e, got_s, got_n, pick,
          up_send, up_recv, dn_send, dn_recv, we_send, we_recv, home) = refs
@@ -655,17 +674,21 @@
 
     if first:
         send_z(0)
+        send_z(1)
         lift(0)
-        send_z(1)
-        lift(1)
         send_z(2)
         send_z(3)
+        lift(1)
+        for p in range(4, PARTS):
+            send_z(p)
         send_y(0)
+        send_y(1)
         descend(0)
-        send_y(1)
-        descend(1)
         send_y(2)
         send_y(3)
+        descend(1)
+        for p in range(4, PARTS):
+            send_y(p)
     else:
         to_e = remote(e_ref, from_w, we_send.at[0], we_recv.at[0], (lat, lax.rem(lon + 1, count)))
         to_w = remote(w_ref, from_e, we_send.at[1], we_recv.at[1], (lat, lax.rem(lon + count - 1, count)))

time: 265 us -> 268 us (1.011)
    pallas_call x1, Pallas kernels: 9.58 us -> 13.9 us  [package(): pl.pallas_call(package_kernel, grid_spec=pltpu.PrefetchScalarGridSpec(num...]
  transfers between devices with their start and end apart: 8 -> 8, of which waited for: 4 -> 4; matrix products, arithmetic and copies ran while one was open for 0% -> 0% of each run, Pallas kernels for 27% -> 28%
where the time goes in v2:
time: 268 us; the launch traced here: 264 us
  Pallas kernels  209 us (78%)
  blocking collectives  18.4 us (7%)
  waiting for transfers between devices  18.1 us (7%)
  starting transfers between devices  12.4 us (5%)
  local copies, waits for them, and re-layouts  3.52 us (1%)
    pallas_call x2, Pallas kernels, halo(): pl.pallas_call(functools.partial(halo_kernel, first), in_specs=[pl.BlockS...  105 us
    pallas_call x2, Pallas kernels, step(): pl.pallas_call(last_kernel if last else first_kernel, grid_spec=pltpu.Pre...  66.8 us
    all_to_all x1, blocking collectives, swap(): return lax.all_to_all(x, 'lon', split_axis=0, concat_axis=0, tiled=True)  18.4 us
    ppermute x8, waiting for transfers between devices, shift(): return lax.ppermute(x, axis, [(i, (i + by) % n) for i in range(n)])  18.1 us
    pallas_call x1, Pallas kernels, package(): pl.pallas_call(package_kernel, grid_spec=pltpu.PrefetchScalarGridSpec(num...  13.9 us
    ppermute x8, starting transfers between devices, shift(): return lax.ppermute(x, axis, [(i, (i + by) % n) for i in range(n)])  12.4 us
    pallas_call x1, Pallas kernels, pack(): pl.pallas_call(pack_kernel, grid_spec=pltpu.PrefetchScalarGridSpec(num_sc...  8.72 us
    pallas_call x1, Pallas kernels, coarse(): pl.pallas_call(coarse_kernel, grid=(SIDE // 2,), in_specs=[pl.BlockSpec((...  7.39 us
  transfers between devices with their start and end apart: 8, of which 4 were waited for; matrix products, arithmetic and copies ran while one was open for 0% of the time, Pallas kernels for 28%

profile of v2, /device:TPU:2, one launch (start us, length us, event | category | flops | bytes accessed | tf_op | source)
XLA Modules:
  0.0 263.9 jit_solution(14229743630630398839)
XLA Ops:
  0.6 0.7 convert_element_type.7
  1.3 0.7 convert_element_type.6.wet
  2.0 6.6 %collective-permute-start.3 = (f32[17,128]{1,0:T(8,128)S(1)}, f32[17,128]{1,0:T(8,128)S(1)}, u32[]{:S(2)}, u32[]{:S(2)}) collective-permute-start(f32[17,128]{1,0:T(8,128)S(1)} %pad_maximum_fusion.base), channel_id=1, source_target_pairs={{0,15},{1,0},{2,1},{3,2},{4,3},{5,4},{6,5},{7,6},{8,7},{9,8},{10,9... | collective-permute-start | bytes 26120 | tf_op jit(solution)/shard_map/ppermute | solution.py:916
  8.6 0.5 collective-permute-start
  9.1 0.9 collective-permute-done.3.east
  10.0 5.6 %collective-permute-done.2.west = f32[17,128]{1,0:T(8,128)S(1)} collective-permute-done((f32[17,128]{1,0:T(8,128)S(1)}, f32[17,128]{1,0:T(8,128)S(1)}, u32[]{:S(2)}, u32[]{:S(2)}) %collective-permute-start.2) | collective-permute-done | bytes 8736 | tf_op jit(solution)/shard_map/ppermute | solution.py:916
  15.6 0.6 copy-done.7
  16.2 0.6 copy-done.9
  16.8 1.9 prep.1
  18.7 7.4 %coarse.1 = (f32[16,224,128]{2,1,0:T(8,128)}, f32[48,128]{1,0:T(8,128)}) custom-call(bf16[48,144,384]{2,1,0:T(8,128)(2,1)} %bitcast.14, bf16[16,48,128]{2,1,0:T(8,128)(2,1)} %bitcast.19, f32[16,8,128]{2,1,0:T(8,128)} %bitcast.20), custom_call_target="tpu_custom_call" | custom-call | flops 1000000000 | bytes 8000000 | tf_op jit(solution)/shard_map/coarse/pallas_call | solution.py:456
  26.1 8.7 %pack.1 = (f32[8,2,2,72,128]{4,3,2,1,0:T(8,128)}, f32[4,144,256]{2,1,0:T(8,128)}, f32[4,144,256]{2,1,0:T(8,128)}) custom-call(s32[8,128]{1,0:T(8,128)} %get-tuple-element.30.tab, f32[8,1152,256]{2,1,0:T(8,128)} %c_ref.3), custom_call_target="tpu_custom_call" | custom-call | flops 10000000 | bytes 12000000 | tf_op jit(solution)/shard_map/pack/pallas_call | solution.py:117
  34.8 5.3 %collective-permute-start.7 = (f32[4,144,256]{2,1,0:T(8,128)}, f32[4,144,256]{2,1,0:T(8,128)S(1)}, u32[]{:S(2)}, u32[]{:S(2)}) collective-permute-start(f32[4,144,256]{2,1,0:T(8,128)} %get-tuple-element.40), channel_id=1, source_target_pairs={{0,15},{1,0},{2,1},{3,2},{4,3},{5,4},{6,5},{7,6},{8,7},{9,8},{10,9... | collective-permute-start | bytes 1769480 | tf_op jit(solution)/shard_map/ppermute | solution.py:916
  40.1 0.7 slice_bitcast_fusion
  40.9 3.2 %collective-permute-done.5.row_ref = f32[48,128]{1,0:T(8,128)S(1)} collective-permute-done((f32[48,128]{1,0:T(8,128)S(1)}, f32[48,128]{1,0:T(8,128)S(1)}, u32[]{:S(2)}, u32[]{:S(2)}) %collective-permute-start.5) | collective-permute-done | bytes 24608 | tf_op jit(solution)/shard_map/ppermute | solution.py:916
  44.1 8.4 %collective-permute-done.4.col_ref = f32[48,128]{1,0:T(8,128)S(1)} collective-permute-done((f32[48,128]{1,0:T(8,128)S(1)}, f32[48,128]{1,0:T(8,128)S(1)}, u32[]{:S(2)}, u32[]{:S(2)}) %collective-permute-start.4) | collective-permute-done | bytes 24608 | tf_op jit(solution)/shard_map/ppermute | solution.py:916
  52.5 0.6 copy-done.5
  53.1 13.9 %package.1 = f32[8,224,256]{2,1,0:T(8,128)} custom-call(s32[8,128]{1,0:T(8,128)} %get-tuple-element.30.tab, f32[16,224,128]{2,1,0:T(8,128)} %get-tuple-element.35.y_ref, f32[48,128]{1,0:T(8,128)} %copy-done.5, f32[48,128]{1,0:T(8,128)} %copy-done.4), custom_call_target="tpu_custom_call" | custom-call | flops 10000000 | bytes 4000000 | tf_op jit(solution)/shard_map/package/pallas_call | solution.py:524
  67.0 58.9 %halo_phys.1 = (f32[16,2,72,128]{3,2,1,0:T(8,128)}, f32[4,2,224,256]{3,2,1,0:T(8,128)}) custom-call(s32[16,128]{1,0:T(8,128)} %get-tuple-element.31.refs_0_, f32[16,2,72,128]{3,2,1,0:T(8,128)} %bitcast.18, f32[4,2,224,256]{3,2,1,0:T(8,128)} %bitcast.13), custom_call_target="tpu_custom_call" | custom-call | flops 1000000 | bytes 100000000 | tf_op jit(solution)/shard_map/halo_phys/pallas_call | solution.py:741
  125.9 0.8 copy-done
  126.9 35.2 %first_step.1 = (f32[8,1152,256]{2,1,0:T(8,128)}, f32[8,2,2,72,128]{4,3,2,1,0:T(8,128)}, f32[4,144,256]{2,1,0:T(8,128)}, f32[4,144,256]{2,1,0:T(8,128)}) custom-call(s32[8,128]{1,0:T(8,128)} %get-tuple-element.30.tab, f32[8,1152,256]{2,1,0:T(8,128)} %c_ref.3, f32[8,224,256]{2,1,0:T(8,128)} %bitcast.11, f32[8,2,2,72,128]{4,3,2,1,0:T(8,128)} %bitcast.15, ...), custom_call_target="tpu_custom_call" | custom-call | flops 100000000 | bytes 25000000 | tf_op jit(solution)/shard_map/first_step/pallas_call | solution.py:393
  162.1 46.6 %halo.1 = (f32[16,2,72,128]{3,2,1,0:T(8,128)}, f32[4,144,256]{2,1,0:T(8,128)}, f32[4,144,256]{2,1,0:T(8,128)}) custom-call(s32[16,128]{1,0:T(8,128)} %get-tuple-element.31.refs_0_, f32[16,2,72,128]{3,2,1,0:T(8,128)} %bitcast.17, f32[4,144,256]{2,1,0:T(8,128)} %get-tuple-element.43.refs_2_, f32[4,144,256]{2,1,0:T(8,128)} %get-tuple-element.44.refs_3_), custom_call_target="tpu_custom_call" | custom-call | flops 1000000 | bytes 100000000 | tf_op jit(solution)/shard_map/halo/pallas_call | solution.py:741
  208.7 31.7 %last_step.1 = (f32[8,1152,256]{2,1,0:T(8,128)}, f32[16,48,256]{2,1,0:T(8,128)}) custom-call(s32[8,128]{1,0:T(8,128)} %get-tuple-element.30.tab, f32[8,1152,256]{2,1,0:T(8,128)} %get-tuple-element.41.c_ref, f32[8,224,256]{2,1,0:T(8,128)} %bitcast.12, f32[8,2,2,72,128]{4,3,2,1,0:T(8,128)} %bitcast.16, f32[4,144,256]{2,1,0:T(8,128)} %get-tuple-element.46.west, ...), custom_call_target="tpu_custom_call" | custom-call | flops 100000000 | bytes 25000000 | tf_op jit(solution)/shard_map/last_step/pallas_call | solution.py:393
  240.3 18.4 %all_to_all.5.got = f32[16,48,256]{2,1,0:T(8,128)} all-to-all(f32[16,48,256]{2,1,0:T(8,128)} %get-tuple-element.49), channel_id=1, replica_groups=mesh['lat'=8,'lon'=16] {'lon'}, dimensions={0} | all-to-all | bytes 1572864 | tf_op jit(solution)/shard_map/all_to_all | solution.py:920
  258.7 5.2 %heat.1 = bf16[48,48,384]{2,1,0:T(8,128)(2,1)} custom-call(s32[8,128]{1,0:T(8,128)} %get-tuple-element.30.tab, f32[16,48,256]{2,1,0:T(8,128)} %all_to_all.5.got, f32[16,128]{1,0:T(8,128)} %copy-done.3, f32[48,384]{1,0:T(8,128)} %light.3), custom_call_target="tpu_custom_call" | custom-call | flops 1000000000 | bytes 3000000 | tf_op jit(solution)/shard_map/heat/pallas_call | solution.py:784
  (28 shorter events, 0.3 us)
Async XLA Ops:
  2.0 24.1 %copy-start.3 = (f32[16,128]{1,0:T(8,128)}, f32[16,128]{1,0:T(8,128)S(1)}, u32[]{:S(2)}) copy-start(f32[16,128]{1,0:T(8,128)S(1)} %convert_element_type.6.wet) | copy-start | bytes 24580
  2.0 13.6 %copy-start.2 = (f32[17,128]{1,0:T(8,128)}, f32[17,128]{1,0:T(8,128)S(1)}, u32[]{:S(2)}) copy-start(f32[17,128]{1,0:T(8,128)S(1)} %pad_maximum_fusion.base) | copy-start | bytes 26116
  2.0 8.0 %collective-permute-start.3 = (f32[17,128]{1,0:T(8,128)S(1)}, f32[17,128]{1,0:T(8,128)S(1)}, u32[]{:S(2)}, u32[]{:S(2)}) collective-permute-start(f32[17,128]{1,0:T(8,128)S(1)} %pad_maximum_fusion.base), channel_id=1, source_target_pairs={{0,15},{1,0},{2,1},{3,2},{4,3},{5,4},{6,5},{7,6},{8,7},{9,8},{10,9... | collective-permute-start | bytes 26120 | tf_op jit(solution)/shard_map/ppermute | solution.py:916
  8.6 7.0 %collective-permute-start.2 = (f32[17,128]{1,0:T(8,128)S(1)}, f32[17,128]{1,0:T(8,128)S(1)}, u32[]{:S(2)}, u32[]{:S(2)}) collective-permute-start(f32[17,128]{1,0:T(8,128)S(1)} %pad_maximum_fusion.base), channel_id=1, source_target_pairs={{0,1},{1,2},{2,3},{3,4},{4,5},{5,6},{6,7},{7,8},{8,9},{9,10},{10,1... | collective-permute-start | bytes 26120 | tf_op jit(solution)/shard_map/ppermute | solution.py:916
  8.6 7.0 %collective-permute-start.1 = (f32[17,128]{1,0:T(8,128)S(1)}, f32[17,128]{1,0:T(8,128)S(1)}, u32[]{:S(2)}, u32[]{:S(2)}) collective-permute-start(f32[17,128]{1,0:T(8,128)S(1)} %pad_maximum_fusion.base), channel_id=1, source_target_pairs={{0,112},{16,0},{32,16},{48,32},{64,48},{80,64},{96,80},{112,96},{1... | collective-permute-start | bytes 26120 | tf_op jit(solution)/shard_map/ppermute | solution.py:916
  8.6 7.0 %collective-permute-start = (f32[17,128]{1,0:T(8,128)S(1)}, f32[17,128]{1,0:T(8,128)S(1)}, u32[]{:S(2)}, u32[]{:S(2)}) collective-permute-start(f32[17,128]{1,0:T(8,128)S(1)} %pad_maximum_fusion.base), channel_id=1, source_target_pairs={{0,16},{16,32},{32,48},{48,64},{64,80},{80,96},{96,112},{112,0},{1... | collective-permute-start | bytes 26120 | tf_op jit(solution)/shard_map/ppermute | solution.py:916
  10.0 5.6 %copy-start.6 = (f32[17,128]{1,0:T(8,128)}, f32[17,128]{1,0:T(8,128)S(1)}, u32[]{:S(2)}) copy-start(f32[17,128]{1,0:T(8,128)S(1)} %collective-permute-done.3.east) | copy-start | bytes 26116
  15.6 0.6 copy-start.7
  15.6 0.6 copy-start.8
  16.2 0.6 copy-start.9
  26.1 14.8 %copy-start.10 = (f32[48,128]{1,0:T(8,128)S(1)}, f32[48,128]{1,0:T(8,128)}, u32[]{:S(2)}) copy-start(f32[48,128]{1,0:T(8,128)} %get-tuple-element.36) | copy-start | bytes 73732
  34.8 91.1 %collective-permute-start.6 = (f32[4,144,256]{2,1,0:T(8,128)}, f32[4,144,256]{2,1,0:T(8,128)S(1)}, u32[]{:S(2)}, u32[]{:S(2)}) collective-permute-start(f32[4,144,256]{2,1,0:T(8,128)} %get-tuple-element.39), channel_id=1, source_target_pairs={{0,1},{1,2},{2,3},{3,4},{4,5},{5,6},{6,7},{7,8},{8,9},{9,10},{10,1... | collective-permute-start | bytes 1769480 | tf_op jit(solution)/shard_map/ppermute | solution.py:916
  34.8 91.1 %collective-permute-start.7 = (f32[4,144,256]{2,1,0:T(8,128)}, f32[4,144,256]{2,1,0:T(8,128)S(1)}, u32[]{:S(2)}, u32[]{:S(2)}) collective-permute-start(f32[4,144,256]{2,1,0:T(8,128)} %get-tuple-element.40), channel_id=1, source_target_pairs={{0,15},{1,0},{2,1},{3,2},{4,3},{5,4},{6,5},{7,6},{8,7},{9,8},{10,9... | collective-permute-start | bytes 1769480 | tf_op jit(solution)/shard_map/ppermute | solution.py:916
  40.9 3.3 %collective-permute-start.5 = (f32[48,128]{1,0:T(8,128)S(1)}, f32[48,128]{1,0:T(8,128)S(1)}, u32[]{:S(2)}, u32[]{:S(2)}) collective-permute-start(f32[48,128]{1,0:T(8,128)S(1)} %slice_bitcast_fusion), channel_id=1, source_target_pairs={{0,16},{16,32},{32,48},{48,64},{64,80},{80,96},{96,112},{112,0},{1... | collective-permute-start | bytes 73736 | tf_op jit(solution)/shard_map/ppermute | solution.py:916
  40.9 11.6 %collective-permute-start.4 = (f32[48,128]{1,0:T(8,128)S(1)}, f32[48,128]{1,0:T(8,128)S(1)}, u32[]{:S(2)}, u32[]{:S(2)}) collective-permute-start(f32[48,128]{1,0:T(8,128)S(1)} %copy-done.10), channel_id=1, source_target_pairs={{0,1},{1,2},{2,3},{3,4},{4,5},{5,6},{6,7},{7,8},{8,9},{9,10},{10,1... | collective-permute-start | bytes 73736 | tf_op jit(solution)/shard_map/ppermute | solution.py:916
  44.1 8.4 %copy-start.4 = (f32[48,128]{1,0:T(8,128)}, f32[48,128]{1,0:T(8,128)S(1)}, u32[]{:S(2)}) copy-start(f32[48,128]{1,0:T(8,128)S(1)} %collective-permute-done.5.row_ref) | copy-start | bytes 73732
  52.5 0.6 copy-start.5
  125.9 0.8 copy-start
  125.9 1.0 copy-start.1

commit v3 on v1

--- a/solution.py
+++ b/solution.py
@@ -477,6 +477,7 @@
 
 def package_kernel(tab, y_ref, col_ref, row_ref, out):
     group = lax.broadcasted_iota(jnp.int32, (8, 128), 1) // SIDE
+    places = [tab[k, 7] for k in range(TILE)]
 
     def chunk(i, carry):
         at = pl.ds(pl.multiple_of(8 * i, 8), 8)
@@ -491,10 +492,15 @@
                     vals[g] = jnp.where(lower, a, roll(b, 16 * d))
                     vals[g + d] = jnp.where(lower, roll(a, 128 - 16 * d), b)
             for k in range(TILE):
-                out[tab[k, 7], at, 128 * h:128 * h + 128] = vals[k]
+                out[places[k], at, 128 * h:128 * h + 128] = vals[k]
         return carry
 
-    lax.fori_loop(0, 25, chunk, 0)
+    def chunks(i, carry):
+        for c in range(5):
+            chunk(5 * i + c, carry)
+        return carry
+
+    lax.fori_loop(0, 5, chunks, 0)
     i = lax.broadcasted_iota(jnp.int32, (256, 128), 0)
     j = lax.broadcasted_iota(jnp.int32, (256, 128), 1)
     last = (i == SIDE * j + SIDE - 1).astype(jnp.float32)
@@ -529,7 +535,7 @@
                                         device_id=where, device_id_type=MESH)
 
 
-PARTS = 4
+PARTS = 7
 PART = PHYS // PARTS
 ORDER = (0, 5, 10, 15, 4, 1, 8, 2, 12, 3, 6, 9, 7, 13, 11, 14)
 
@@ -544,9 +550,9 @@
 
 def halo_kernel(first, *refs):
     if first:
-        (tab, up_ref, phys, rows_ref, phys_out, got_s, got_n, pick, turn, mid0, mid1, mid2, mid3,
-         up_send, up_recv, dn_send, dn_recv, z_send, z_recv, y_send, y_recv, own, rest, home) = refs
-        mid = (mid0, mid1, mid2, mid3)
+        tab, up_ref, phys, rows_ref, phys_out, got_s, got_n, pick, turn = refs[:9]
+        mid = refs[9:9 + PARTS]
+        (up_send, up_recv, dn_send, dn_recv, z_send, z_recv, y_send, y_recv, own, rest, home) = refs[9 + PARTS:]
     else:
         (tab, up_ref, w_ref, e_ref, rows_ref, from_w, from_e, got_s, got_n, pick,
          up_send, up_recv, dn_send, dn_recv, we_send, we_recv, home) = refs
@@ -655,17 +661,21 @@
 
     if first:
         send_z(0)
+        send_z(1)
         lift(0)
-        send_z(1)
-        lift(1)
         send_z(2)
         send_z(3)
+        lift(1)
+        for p in range(4, PARTS):
+            send_z(p)
         send_y(0)
+        send_y(1)
         descend(0)
-        send_y(1)
-        descend(1)
         send_y(2)
         send_y(3)
+        descend(1)
+        for p in range(4, PARTS):
+            send_y(p)
     else:
         to_e = remote(e_ref, from_w, we_send.at[0], we_recv.at[0], (lat, lax.rem(lon + 1, count)))
         to_w = remote(w_ref, from_e, we_send.at[1], we_recv.at[1], (lat, lax.rem(lon + count - 1, count)))

time: 265 us -> 261 us (0.985)
  Pallas kernels: 207 us -> 202 us
    pallas_call x1, Pallas kernels: 9.58 us -> 6.41 us  [package(): pl.pallas_call(package_kernel, in_specs=[pl.BlockSpec(memory_space=pltpu....]
  transfers between devices with their start and end apart: 8 -> 8, of which waited for: 4 -> 4; matrix products, arithmetic and copies ran while one was open for 0% -> 0% of each run, Pallas kernels for 27% -> 25%
where the time goes in v3:
time: 261 us; the launch traced here: 256 us
  Pallas kernels  202 us (77%)
  blocking collectives  18.4 us (7%)
  waiting for transfers between devices  18.1 us (7%)
  starting transfers between devices  12.4 us (5%)
  local copies, waits for them, and re-layouts  3.52 us (1%)
    pallas_call x2, Pallas kernels, halo(): pl.pallas_call(functools.partial(halo_kernel, first), in_specs=[pl.BlockS...  105 us
    pallas_call x2, Pallas kernels, step(): pl.pallas_call(last_kernel if last else first_kernel, grid_spec=pltpu.Pre...  66.8 us
    all_to_all x1, blocking collectives, swap(): return lax.all_to_all(x, 'lon', split_axis=0, concat_axis=0, tiled=True)  18.4 us
    ppermute x8, waiting for transfers between devices, shift(): return lax.ppermute(x, axis, [(i, (i + by) % n) for i in range(n)])  18.1 us
    ppermute x8, starting transfers between devices, shift(): return lax.ppermute(x, axis, [(i, (i + by) % n) for i in range(n)])  12.4 us
    pallas_call x1, Pallas kernels, pack(): pl.pallas_call(pack_kernel, grid_spec=pltpu.PrefetchScalarGridSpec(num_sc...  8.75 us
    pallas_call x1, Pallas kernels, coarse(): pl.pallas_call(coarse_kernel, grid=(SIDE // 2,), in_specs=[pl.BlockSpec((...  7.35 us
    pallas_call x1, Pallas kernels, package(): pl.pallas_call(package_kernel, in_specs=[pl.BlockSpec(memory_space=pltpu....  6.41 us
  transfers between devices with their start and end apart: 8, of which 4 were waited for; matrix products, arithmetic and copies ran while one was open for 0% of the time, Pallas kernels for 25%

profile of v3, /device:TPU:2, one launch (start us, length us, event | category | flops | bytes accessed | tf_op | source)
XLA Modules:
  0.0 256.4 jit_solution(2233181189355374260)
XLA Ops:
  0.6 0.7 convert_element_type.7
  1.3 0.7 convert_element_type.6.wet
  2.0 6.6 %collective-permute-start.3 = (f32[17,128]{1,0:T(8,128)S(1)}, f32[17,128]{1,0:T(8,128)S(1)}, u32[]{:S(2)}, u32[]{:S(2)}) collective-permute-start(f32[17,128]{1,0:T(8,128)S(1)} %pad_maximum_fusion.base), channel_id=1, source_target_pairs={{0,15},{1,0},{2,1},{3,2},{4,3},{5,4},{6,5},{7,6},{8,7},{9,8},{10,9... | collective-permute-start | bytes 26120 | tf_op jit(solution)/shard_map/ppermute | solution.py:903
  8.6 0.5 collective-permute-start
  9.1 0.9 collective-permute-done.3.east
  10.0 5.6 %collective-permute-done.2.west = f32[17,128]{1,0:T(8,128)S(1)} collective-permute-done((f32[17,128]{1,0:T(8,128)S(1)}, f32[17,128]{1,0:T(8,128)S(1)}, u32[]{:S(2)}, u32[]{:S(2)}) %collective-permute-start.2) | collective-permute-done | bytes 8736 | tf_op jit(solution)/shard_map/ppermute | solution.py:903
  15.6 0.6 copy-done.7
  16.2 0.6 copy-done.9
  16.8 1.9 prep.1
  18.7 7.4 %coarse.1 = (f32[16,200,128]{2,1,0:T(8,128)}, f32[48,128]{1,0:T(8,128)}) custom-call(bf16[48,144,384]{2,1,0:T(8,128)(2,1)} %bitcast.14, bf16[16,48,128]{2,1,0:T(8,128)(2,1)} %bitcast.19, f32[16,8,128]{2,1,0:T(8,128)} %bitcast.20), custom_call_target="tpu_custom_call" | custom-call | flops 1000000000 | bytes 8000000 | tf_op jit(solution)/shard_map/coarse/pallas_call | solution.py:456
  26.0 8.8 %pack.1 = (f32[8,2,2,72,128]{4,3,2,1,0:T(8,128)}, f32[4,144,256]{2,1,0:T(8,128)}, f32[4,144,256]{2,1,0:T(8,128)}) custom-call(s32[8,128]{1,0:T(8,128)} %get-tuple-element.30.tab, f32[8,1152,256]{2,1,0:T(8,128)} %c_ref.3), custom_call_target="tpu_custom_call" | custom-call | flops 10000000 | bytes 12000000 | tf_op jit(solution)/shard_map/pack/pallas_call | solution.py:117
  34.8 5.3 %collective-permute-start.7 = (f32[4,144,256]{2,1,0:T(8,128)}, f32[4,144,256]{2,1,0:T(8,128)S(1)}, u32[]{:S(2)}, u32[]{:S(2)}) collective-permute-start(f32[4,144,256]{2,1,0:T(8,128)} %get-tuple-element.40), channel_id=1, source_target_pairs={{0,15},{1,0},{2,1},{3,2},{4,3},{5,4},{6,5},{7,6},{8,7},{9,8},{10,9... | collective-permute-start | bytes 1769480 | tf_op jit(solution)/shard_map/ppermute | solution.py:903
  40.1 0.7 slice_bitcast_fusion
  40.9 3.2 %collective-permute-done.5.row_ref = f32[48,128]{1,0:T(8,128)S(1)} collective-permute-done((f32[48,128]{1,0:T(8,128)S(1)}, f32[48,128]{1,0:T(8,128)S(1)}, u32[]{:S(2)}, u32[]{:S(2)}) %collective-permute-start.5) | collective-permute-done | bytes 24608 | tf_op jit(solution)/shard_map/ppermute | solution.py:903
  44.1 8.4 %collective-permute-done.4.col_ref = f32[48,128]{1,0:T(8,128)S(1)} collective-permute-done((f32[48,128]{1,0:T(8,128)S(1)}, f32[48,128]{1,0:T(8,128)S(1)}, u32[]{:S(2)}, u32[]{:S(2)}) %collective-permute-start.4) | collective-permute-done | bytes 24608 | tf_op jit(solution)/shard_map/ppermute | solution.py:903
  52.5 0.6 copy-done.5
  53.1 6.4 %package.1 = f32[8,224,256]{2,1,0:T(8,128)} custom-call(s32[8,128]{1,0:T(8,128)} %get-tuple-element.30.tab, f32[16,200,128]{2,1,0:T(8,128)} %get-tuple-element.35.y_ref, f32[48,128]{1,0:T(8,128)} %copy-done.5, f32[48,128]{1,0:T(8,128)} %copy-done.4), custom_call_target="tpu_custom_call" | custom-call | flops 10000000 | bytes 4000000 | tf_op jit(solution)/shard_map/package/pallas_call | solution.py:520
  59.5 58.9 %halo_phys.1 = (f32[16,2,72,128]{3,2,1,0:T(8,128)}, f32[4,2,224,256]{3,2,1,0:T(8,128)}) custom-call(s32[16,128]{1,0:T(8,128)} %get-tuple-element.31.refs_0_, f32[16,2,72,128]{3,2,1,0:T(8,128)} %bitcast.18, f32[4,2,224,256]{3,2,1,0:T(8,128)} %bitcast.13), custom_call_target="tpu_custom_call" | custom-call | flops 1000000 | bytes 100000000 | tf_op jit(solution)/shard_map/halo_phys/pallas_call | solution.py:728
  118.4 0.8 copy-done
  119.4 35.2 %first_step.1 = (f32[8,1152,256]{2,1,0:T(8,128)}, f32[8,2,2,72,128]{4,3,2,1,0:T(8,128)}, f32[4,144,256]{2,1,0:T(8,128)}, f32[4,144,256]{2,1,0:T(8,128)}) custom-call(s32[8,128]{1,0:T(8,128)} %get-tuple-element.30.tab, f32[8,1152,256]{2,1,0:T(8,128)} %c_ref.3, f32[8,224,256]{2,1,0:T(8,128)} %bitcast.11, f32[8,2,2,72,128]{4,3,2,1,0:T(8,128)} %bitcast.15, ...), custom_call_target="tpu_custom_call" | custom-call | flops 100000000 | bytes 25000000 | tf_op jit(solution)/shard_map/first_step/pallas_call | solution.py:393
  154.6 46.6 %halo.1 = (f32[16,2,72,128]{3,2,1,0:T(8,128)}, f32[4,144,256]{2,1,0:T(8,128)}, f32[4,144,256]{2,1,0:T(8,128)}) custom-call(s32[16,128]{1,0:T(8,128)} %get-tuple-element.31.refs_0_, f32[16,2,72,128]{3,2,1,0:T(8,128)} %bitcast.17, f32[4,144,256]{2,1,0:T(8,128)} %get-tuple-element.43.refs_2_, f32[4,144,256]{2,1,0:T(8,128)} %get-tuple-element.44.refs_3_), custom_call_target="tpu_custom_call" | custom-call | flops 1000000 | bytes 100000000 | tf_op jit(solution)/shard_map/halo/pallas_call | solution.py:728
  201.2 31.7 %last_step.1 = (f32[8,1152,256]{2,1,0:T(8,128)}, f32[16,48,256]{2,1,0:T(8,128)}) custom-call(s32[8,128]{1,0:T(8,128)} %get-tuple-element.30.tab, f32[8,1152,256]{2,1,0:T(8,128)} %get-tuple-element.41.c_ref, f32[8,224,256]{2,1,0:T(8,128)} %bitcast.12, f32[8,2,2,72,128]{4,3,2,1,0:T(8,128)} %bitcast.16, f32[4,144,256]{2,1,0:T(8,128)} %get-tuple-element.46.west, ...), custom_call_target="tpu_custom_call" | custom-call | flops 100000000 | bytes 25000000 | tf_op jit(solution)/shard_map/last_step/pallas_call | solution.py:393
  232.9 18.4 %all_to_all.5.got = f32[16,48,256]{2,1,0:T(8,128)} all-to-all(f32[16,48,256]{2,1,0:T(8,128)} %get-tuple-element.49), channel_id=1, replica_groups=mesh['lat'=8,'lon'=16] {'lon'}, dimensions={0} | all-to-all | bytes 1572864 | tf_op jit(solution)/shard_map/all_to_all | solution.py:907
  251.2 5.2 %heat.1 = bf16[48,48,384]{2,1,0:T(8,128)(2,1)} custom-call(s32[8,128]{1,0:T(8,128)} %get-tuple-element.30.tab, f32[16,48,256]{2,1,0:T(8,128)} %all_to_all.5.got, f32[16,128]{1,0:T(8,128)} %copy-done.3, f32[48,384]{1,0:T(8,128)} %light.3), custom_call_target="tpu_custom_call" | custom-call | flops 1000000000 | bytes 3000000 | tf_op jit(solution)/shard_map/heat/pallas_call | solution.py:771
  (28 shorter events, 0.3 us)
Async XLA Ops:
  2.0 24.1 %copy-start.3 = (f32[16,128]{1,0:T(8,128)}, f32[16,128]{1,0:T(8,128)S(1)}, u32[]{:S(2)}) copy-start(f32[16,128]{1,0:T(8,128)S(1)} %convert_element_type.6.wet) | copy-start | bytes 24580
  2.0 13.6 %copy-start.2 = (f32[17,128]{1,0:T(8,128)}, f32[17,128]{1,0:T(8,128)S(1)}, u32[]{:S(2)}) copy-start(f32[17,128]{1,0:T(8,128)S(1)} %pad_maximum_fusion.base) | copy-start | bytes 26116
  2.0 8.0 %collective-permute-start.3 = (f32[17,128]{1,0:T(8,128)S(1)}, f32[17,128]{1,0:T(8,128)S(1)}, u32[]{:S(2)}, u32[]{:S(2)}) collective-permute-start(f32[17,128]{1,0:T(8,128)S(1)} %pad_maximum_fusion.base), channel_id=1, source_target_pairs={{0,15},{1,0},{2,1},{3,2},{4,3},{5,4},{6,5},{7,6},{8,7},{9,8},{10,9... | collective-permute-start | bytes 26120 | tf_op jit(solution)/shard_map/ppermute | solution.py:903
  8.6 7.0 %collective-permute-start.2 = (f32[17,128]{1,0:T(8,128)S(1)}, f32[17,128]{1,0:T(8,128)S(1)}, u32[]{:S(2)}, u32[]{:S(2)}) collective-permute-start(f32[17,128]{1,0:T(8,128)S(1)} %pad_maximum_fusion.base), channel_id=1, source_target_pairs={{0,1},{1,2},{2,3},{3,4},{4,5},{5,6},{6,7},{7,8},{8,9},{9,10},{10,1... | collective-permute-start | bytes 26120 | tf_op jit(solution)/shard_map/ppermute | solution.py:903
  8.6 7.0 %collective-permute-start.1 = (f32[17,128]{1,0:T(8,128)S(1)}, f32[17,128]{1,0:T(8,128)S(1)}, u32[]{:S(2)}, u32[]{:S(2)}) collective-permute-start(f32[17,128]{1,0:T(8,128)S(1)} %pad_maximum_fusion.base), channel_id=1, source_target_pairs={{0,112},{16,0},{32,16},{48,32},{64,48},{80,64},{96,80},{112,96},{1... | collective-permute-start | bytes 26120 | tf_op jit(solution)/shard_map/ppermute | solution.py:903
  8.6 7.0 %collective-permute-start = (f32[17,128]{1,0:T(8,128)S(1)}, f32[17,128]{1,0:T(8,128)S(1)}, u32[]{:S(2)}, u32[]{:S(2)}) collective-permute-start(f32[17,128]{1,0:T(8,128)S(1)} %pad_maximum_fusion.base), channel_id=1, source_target_pairs={{0,16},{16,32},{32,48},{48,64},{64,80},{80,96},{96,112},{112,0},{1... | collective-permute-start | bytes 26120 | tf_op jit(solution)/shard_map/ppermute | solution.py:903
  10.0 5.6 %copy-start.6 = (f32[17,128]{1,0:T(8,128)}, f32[17,128]{1,0:T(8,128)S(1)}, u32[]{:S(2)}) copy-start(f32[17,128]{1,0:T(8,128)S(1)} %collective-permute-done.3.east) | copy-start | bytes 26116
  15.6 0.6 copy-start.7
  15.6 0.6 copy-start.8
  16.2 0.6 copy-start.9
  26.0 14.8 %copy-start.10 = (f32[48,128]{1,0:T(8,128)S(1)}, f32[48,128]{1,0:T(8,128)}, u32[]{:S(2)}) copy-start(f32[48,128]{1,0:T(8,128)} %get-tuple-element.36) | copy-start | bytes 73732
  34.8 83.6 %collective-permute-start.6 = (f32[4,144,256]{2,1,0:T(8,128)}, f32[4,144,256]{2,1,0:T(8,128)S(1)}, u32[]{:S(2)}, u32[]{:S(2)}) collective-permute-start(f32[4,144,256]{2,1,0:T(8,128)} %get-tuple-element.39), channel_id=1, source_target_pairs={{0,1},{1,2},{2,3},{3,4},{4,5},{5,6},{6,7},{7,8},{8,9},{9,10},{10,1... | collective-permute-start | bytes 1769480 | tf_op jit(solution)/shard_map/ppermute | solution.py:903
  34.8 83.6 %collective-permute-start.7 = (f32[4,144,256]{2,1,0:T(8,128)}, f32[4,144,256]{2,1,0:T(8,128)S(1)}, u32[]{:S(2)}, u32[]{:S(2)}) collective-permute-start(f32[4,144,256]{2,1,0:T(8,128)} %get-tuple-element.40), channel_id=1, source_target_pairs={{0,15},{1,0},{2,1},{3,2},{4,3},{5,4},{6,5},{7,6},{8,7},{9,8},{10,9... | collective-permute-start | bytes 1769480 | tf_op jit(solution)/shard_map/ppermute | solution.py:903
  40.9 3.3 %collective-permute-start.5 = (f32[48,128]{1,0:T(8,128)S(1)}, f32[48,128]{1,0:T(8,128)S(1)}, u32[]{:S(2)}, u32[]{:S(2)}) collective-permute-start(f32[48,128]{1,0:T(8,128)S(1)} %slice_bitcast_fusion), channel_id=1, source_target_pairs={{0,16},{16,32},{32,48},{48,64},{64,80},{80,96},{96,112},{112,0},{1... | collective-permute-start | bytes 73736 | tf_op jit(solution)/shard_map/ppermute | solution.py:903
  40.9 11.6 %collective-permute-start.4 = (f32[48,128]{1,0:T(8,128)S(1)}, f32[48,128]{1,0:T(8,128)S(1)}, u32[]{:S(2)}, u32[]{:S(2)}) collective-permute-start(f32[48,128]{1,0:T(8,128)S(1)} %copy-done.10), channel_id=1, source_target_pairs={{0,1},{1,2},{2,3},{3,4},{4,5},{5,6},{6,7},{7,8},{8,9},{9,10},{10,1... | collective-permute-start | bytes 73736 | tf_op jit(solution)/shard_map/ppermute | solution.py:903
  44.1 8.4 %copy-start.4 = (f32[48,128]{1,0:T(8,128)}, f32[48,128]{1,0:T(8,128)S(1)}, u32[]{:S(2)}) copy-start(f32[48,128]{1,0:T(8,128)S(1)} %collective-permute-done.5.row_ref) | copy-start | bytes 73732
  52.5 0.6 copy-start.5
  118.4 0.8 copy-start
  118.4 1.0 copy-start.1

commit v4 on v3

--- a/solution.py
+++ b/solution.py
@@ -327,26 +327,25 @@
     absorb = 0.04 + 0.02 * (pos(out[0, 480:528, :]) + pos(out[0, 528:576, :]))
     above = depth(absorb)
     par_ref[...] = phys[0, 196:197, :] * jnp.exp(-(above + 0.5 * absorb))
-    for h in range(2):
-        wet = jnp.broadcast_to(phys[0, 197:198, H[h]], (8, 128))
-
-        def chunk(i, carry):
-            l0 = pl.multiple_of(i * 8, 8)
-
-            def get(t):
+    wets = [jnp.broadcast_to(phys[0, 197:198, H[h]], (8, 128)) for h in range(2)]
+
+    def chunk(i, carry):
+        l0 = pl.multiple_of(i * 8, 8)
+        for h in range(2):
+
+            def get(t, h=h):
                 return out[0, pl.ds(pl.multiple_of(t * LEV + l0, 8), 8), H[h]]
 
+            def put(t, v, h=h):
+                out[0, pl.ds(pl.multiple_of(t * LEV + l0, 8), 8), H[h]] = v * wets[h]
+
             held = [get(t) for t in range(NTR)]
-
-            def put(t, v):
-                out[0, pl.ds(pl.multiple_of(t * LEV + l0, 8), 8), H[h]] = v * wet
-
             warm = jnp.exp(0.0639 * phys[0, pl.ds(pl.multiple_of(96 + l0, 8), 8), H[h]])
             par = par_ref[pl.ds(l0, 8), H[h]]
-            react(lambda t: held[t], put, par, warm)
-            return carry
-
-        lax.fori_loop(0, LEV // 8, chunk, 0)
+            react(lambda t, held=held: held[t], put, par, warm)
+        return carry
+
+    lax.fori_loop(0, LEV // 8, chunk, 0)
 
 
 def first_kernel(tab, c_ref, phys, rows, west, east, out, rows_out, w_out, e_out, coef, par_ref, cross, along, one, two):

time: 261 us -> 260 us (level)
  transfers between devices with their start and end apart: 8 -> 8, of which waited for: 4 -> 4; matrix products, arithmetic and copies ran while one was open for 0% -> 0% of each run, Pallas kernels for 25% -> 26%
where the time goes in v4:
time: 260 us; the launch traced here: 256 us
  Pallas kernels  201 us (77%)
  blocking collectives  18.3 us (7%)
  waiting for transfers between devices  18.1 us (7%)
  starting transfers between devices  12.4 us (5%)
  local copies, waits for them, and re-layouts  3.52 us (1%)
    pallas_call x2, Pallas kernels, halo(): pl.pallas_call(functools.partial(halo_kernel, first), in_specs=[pl.BlockS...  105 us
    pallas_call x2, Pallas kernels, step(): pl.pallas_call(last_kernel if last else first_kernel, grid_spec=pltpu.Pre...  66.1 us
    all_to_all x1, blocking collectives, swap(): return lax.all_to_all(x, 'lon', split_axis=0, concat_axis=0, tiled=True)  18.3 us
    ppermute x8, waiting for transfers between devices, shift(): return lax.ppermute(x, axis, [(i, (i + by) % n) for i in range(n)])  18.1 us
    ppermute x8, starting transfers between devices, shift(): return lax.ppermute(x, axis, [(i, (i + by) % n) for i in range(n)])  12.4 us
    pallas_call x1, Pallas kernels, pack(): pl.pallas_call(pack_kernel, grid_spec=pltpu.PrefetchScalarGridSpec(num_sc...  8.75 us
    pallas_call x1, Pallas kernels, coarse(): pl.pallas_call(coarse_kernel, grid=(SIDE // 2,), in_specs=[pl.BlockSpec((...  7.35 us
    pallas_call x1, Pallas kernels, package(): pl.pallas_call(package_kernel, in_specs=[pl.BlockSpec(memory_space=pltpu....  6.41 us
  transfers between devices with their start and end apart: 8, of which 4 were waited for; matrix products, arithmetic and copies ran while one was open for 0% of the time, Pallas kernels for 26%

profile of v4, /device:TPU:2, one launch (start us, length us, event | category | flops | bytes accessed | tf_op | source)
XLA Modules:
  0.0 255.7 jit_solution(5999421726189479105)
XLA Ops:
  0.6 0.7 convert_element_type.7
  1.3 0.7 convert_element_type.6.wet
  2.0 6.6 %collective-permute-start.3 = (f32[17,128]{1,0:T(8,128)S(1)}, f32[17,128]{1,0:T(8,128)S(1)}, u32[]{:S(2)}, u32[]{:S(2)}) collective-permute-start(f32[17,128]{1,0:T(8,128)S(1)} %pad_maximum_fusion.base), channel_id=1, source_target_pairs={{0,15},{1,0},{2,1},{3,2},{4,3},{5,4},{6,5},{7,6},{8,7},{9,8},{10,9... | collective-permute-start | bytes 26120 | tf_op jit(solution)/shard_map/ppermute | solution.py:902
  8.6 0.5 collective-permute-start
  9.1 0.9 collective-permute-done.3.east
  10.0 5.6 %collective-permute-done.2.west = f32[17,128]{1,0:T(8,128)S(1)} collective-permute-done((f32[17,128]{1,0:T(8,128)S(1)}, f32[17,128]{1,0:T(8,128)S(1)}, u32[]{:S(2)}, u32[]{:S(2)}) %collective-permute-start.2) | collective-permute-done | bytes 8736 | tf_op jit(solution)/shard_map/ppermute | solution.py:902
  15.6 0.6 copy-done.7
  16.2 0.6 copy-done.9
  16.8 1.9 prep.1
  18.7 7.4 %coarse.1 = (f32[16,200,128]{2,1,0:T(8,128)}, f32[48,128]{1,0:T(8,128)}) custom-call(bf16[48,144,384]{2,1,0:T(8,128)(2,1)} %bitcast.14, bf16[16,48,128]{2,1,0:T(8,128)(2,1)} %bitcast.19, f32[16,8,128]{2,1,0:T(8,128)} %bitcast.20), custom_call_target="tpu_custom_call" | custom-call | flops 1000000000 | bytes 8000000 | tf_op jit(solution)/shard_map/coarse/pallas_call | solution.py:455
  26.0 8.8 %pack.1 = (f32[8,2,2,72,128]{4,3,2,1,0:T(8,128)}, f32[4,144,256]{2,1,0:T(8,128)}, f32[4,144,256]{2,1,0:T(8,128)}) custom-call(s32[8,128]{1,0:T(8,128)} %get-tuple-element.30.tab, f32[8,1152,256]{2,1,0:T(8,128)} %c_ref.3), custom_call_target="tpu_custom_call" | custom-call | flops 10000000 | bytes 12000000 | tf_op jit(solution)/shard_map/pack/pallas_call | solution.py:117
  34.8 5.3 %collective-permute-start.7 = (f32[4,144,256]{2,1,0:T(8,128)}, f32[4,144,256]{2,1,0:T(8,128)S(1)}, u32[]{:S(2)}, u32[]{:S(2)}) collective-permute-start(f32[4,144,256]{2,1,0:T(8,128)} %get-tuple-element.40), channel_id=1, source_target_pairs={{0,15},{1,0},{2,1},{3,2},{4,3},{5,4},{6,5},{7,6},{8,7},{9,8},{10,9... | collective-permute-start | bytes 1769480 | tf_op jit(solution)/shard_map/ppermute | solution.py:902
  40.1 0.7 slice_bitcast_fusion
  40.9 3.2 %collective-permute-done.5.row_ref = f32[48,128]{1,0:T(8,128)S(1)} collective-permute-done((f32[48,128]{1,0:T(8,128)S(1)}, f32[48,128]{1,0:T(8,128)S(1)}, u32[]{:S(2)}, u32[]{:S(2)}) %collective-permute-start.5) | collective-permute-done | bytes 24608 | tf_op jit(solution)/shard_map/ppermute | solution.py:902
  44.1 8.4 %collective-permute-done.4.col_ref = f32[48,128]{1,0:T(8,128)S(1)} collective-permute-done((f32[48,128]{1,0:T(8,128)S(1)}, f32[48,128]{1,0:T(8,128)S(1)}, u32[]{:S(2)}, u32[]{:S(2)}) %collective-permute-start.4) | collective-permute-done | bytes 24608 | tf_op jit(solution)/shard_map/ppermute | solution.py:902
  52.5 0.6 copy-done.5
  53.1 6.4 %package.1 = f32[8,224,256]{2,1,0:T(8,128)} custom-call(s32[8,128]{1,0:T(8,128)} %get-tuple-element.30.tab, f32[16,200,128]{2,1,0:T(8,128)} %get-tuple-element.35.y_ref, f32[48,128]{1,0:T(8,128)} %copy-done.5, f32[48,128]{1,0:T(8,128)} %copy-done.4), custom_call_target="tpu_custom_call" | custom-call | flops 10000000 | bytes 4000000 | tf_op jit(solution)/shard_map/package/pallas_call | solution.py:519
  59.5 58.9 %halo_phys.1 = (f32[16,2,72,128]{3,2,1,0:T(8,128)}, f32[4,2,224,256]{3,2,1,0:T(8,128)}) custom-call(s32[16,128]{1,0:T(8,128)} %get-tuple-element.31.refs_0_, f32[16,2,72,128]{3,2,1,0:T(8,128)} %bitcast.18, f32[4,2,224,256]{3,2,1,0:T(8,128)} %bitcast.13), custom_call_target="tpu_custom_call" | custom-call | flops 1000000 | bytes 100000000 | tf_op jit(solution)/shard_map/halo_phys/pallas_call | solution.py:727
  118.4 0.8 copy-done
  119.4 34.8 %first_step.1 = (f32[8,1152,256]{2,1,0:T(8,128)}, f32[8,2,2,72,128]{4,3,2,1,0:T(8,128)}, f32[4,144,256]{2,1,0:T(8,128)}, f32[4,144,256]{2,1,0:T(8,128)}) custom-call(s32[8,128]{1,0:T(8,128)} %get-tuple-element.30.tab, f32[8,1152,256]{2,1,0:T(8,128)} %c_ref.3, f32[8,224,256]{2,1,0:T(8,128)} %bitcast.11, f32[8,2,2,72,128]{4,3,2,1,0:T(8,128)} %bitcast.15, ...), custom_call_target="tpu_custom_call" | custom-call | flops 100000000 | bytes 25000000 | tf_op jit(solution)/shard_map/first_step/pallas_call | solution.py:392
  154.2 46.6 %halo.1 = (f32[16,2,72,128]{3,2,1,0:T(8,128)}, f32[4,144,256]{2,1,0:T(8,128)}, f32[4,144,256]{2,1,0:T(8,128)}) custom-call(s32[16,128]{1,0:T(8,128)} %get-tuple-element.31.refs_0_, f32[16,2,72,128]{3,2,1,0:T(8,128)} %bitcast.17, f32[4,144,256]{2,1,0:T(8,128)} %get-tuple-element.43.refs_2_, f32[4,144,256]{2,1,0:T(8,128)} %get-tuple-element.44.refs_3_), custom_call_target="tpu_custom_call" | custom-call | flops 1000000 | bytes 100000000 | tf_op jit(solution)/shard_map/halo/pallas_call | solution.py:727
  200.8 31.4 %last_step.1 = (f32[8,1152,256]{2,1,0:T(8,128)}, f32[16,48,256]{2,1,0:T(8,128)}) custom-call(s32[8,128]{1,0:T(8,128)} %get-tuple-element.30.tab, f32[8,1152,256]{2,1,0:T(8,128)} %get-tuple-element.41.c_ref, f32[8,224,256]{2,1,0:T(8,128)} %bitcast.12, f32[8,2,2,72,128]{4,3,2,1,0:T(8,128)} %bitcast.16, f32[4,144,256]{2,1,0:T(8,128)} %get-tuple-element.46.west, ...), custom_call_target="tpu_custom_call" | custom-call | flops 100000000 | bytes 25000000 | tf_op jit(solution)/shard_map/last_step/pallas_call | solution.py:392
  232.2 18.3 %all_to_all.5.got = f32[16,48,256]{2,1,0:T(8,128)} all-to-all(f32[16,48,256]{2,1,0:T(8,128)} %get-tuple-element.49), channel_id=1, replica_groups=mesh['lat'=8,'lon'=16] {'lon'}, dimensions={0} | all-to-all | bytes 1572864 | tf_op jit(solution)/shard_map/all_to_all | solution.py:906
  250.5 5.2 %heat.1 = bf16[48,48,384]{2,1,0:T(8,128)(2,1)} custom-call(s32[8,128]{1,0:T(8,128)} %get-tuple-element.30.tab, f32[16,48,256]{2,1,0:T(8,128)} %all_to_all.5.got, f32[16,128]{1,0:T(8,128)} %copy-done.3, f32[48,384]{1,0:T(8,128)} %light.3), custom_call_target="tpu_custom_call" | custom-call | flops 1000000000 | bytes 3000000 | tf_op jit(solution)/shard_map/heat/pallas_call | solution.py:770
  (28 shorter events, 0.3 us)
Async XLA Ops:
  2.0 24.1 %copy-start.3 = (f32[16,128]{1,0:T(8,128)}, f32[16,128]{1,0:T(8,128)S(1)}, u32[]{:S(2)}) copy-start(f32[16,128]{1,0:T(8,128)S(1)} %convert_element_type.6.wet) | copy-start | bytes 24580
  2.0 13.6 %copy-start.2 = (f32[17,128]{1,0:T(8,128)}, f32[17,128]{1,0:T(8,128)S(1)}, u32[]{:S(2)}) copy-start(f32[17,128]{1,0:T(8,128)S(1)} %pad_maximum_fusion.base) | copy-start | bytes 26116
  2.0 8.0 %collective-permute-start.3 = (f32[17,128]{1,0:T(8,128)S(1)}, f32[17,128]{1,0:T(8,128)S(1)}, u32[]{:S(2)}, u32[]{:S(2)}) collective-permute-start(f32[17,128]{1,0:T(8,128)S(1)} %pad_maximum_fusion.base), channel_id=1, source_target_pairs={{0,15},{1,0},{2,1},{3,2},{4,3},{5,4},{6,5},{7,6},{8,7},{9,8},{10,9... | collective-permute-start | bytes 26120 | tf_op jit(solution)/shard_map/ppermute | solution.py:902
  8.6 7.0 %collective-permute-start.2 = (f32[17,128]{1,0:T(8,128)S(1)}, f32[17,128]{1,0:T(8,128)S(1)}, u32[]{:S(2)}, u32[]{:S(2)}) collective-permute-start(f32[17,128]{1,0:T(8,128)S(1)} %pad_maximum_fusion.base), channel_id=1, source_target_pairs={{0,1},{1,2},{2,3},{3,4},{4,5},{5,6},{6,7},{7,8},{8,9},{9,10},{10,1... | collective-permute-start | bytes 26120 | tf_op jit(solution)/shard_map/ppermute | solution.py:902
  8.6 7.0 %collective-permute-start.1 = (f32[17,128]{1,0:T(8,128)S(1)}, f32[17,128]{1,0:T(8,128)S(1)}, u32[]{:S(2)}, u32[]{:S(2)}) collective-permute-start(f32[17,128]{1,0:T(8,128)S(1)} %pad_maximum_fusion.base), channel_id=1, source_target_pairs={{0,112},{16,0},{32,16},{48,32},{64,48},{80,64},{96,80},{112,96},{1... | collective-permute-start | bytes 26120 | tf_op jit(solution)/shard_map/ppermute | solution.py:902
  8.6 7.0 %collective-permute-start = (f32[17,128]{1,0:T(8,128)S(1)}, f32[17,128]{1,0:T(8,128)S(1)}, u32[]{:S(2)}, u32[]{:S(2)}) collective-permute-start(f32[17,128]{1,0:T(8,128)S(1)} %pad_maximum_fusion.base), channel_id=1, source_target_pairs={{0,16},{16,32},{32,48},{48,64},{64,80},{80,96},{96,112},{112,0},{1... | collective-permute-start | bytes 26120 | tf_op jit(solution)/shard_map/ppermute | solution.py:902
  10.0 5.6 %copy-start.6 = (f32[17,128]{1,0:T(8,128)}, f32[17,128]{1,0:T(8,128)S(1)}, u32[]{:S(2)}) copy-start(f32[17,128]{1,0:T(8,128)S(1)} %collective-permute-done.3.east) | copy-start | bytes 26116
  15.6 0.6 copy-start.7
  15.6 0.6 copy-start.8
  16.2 0.6 copy-start.9
  26.0 14.8 %copy-start.10 = (f32[48,128]{1,0:T(8,128)S(1)}, f32[48,128]{1,0:T(8,128)}, u32[]{:S(2)}) copy-start(f32[48,128]{1,0:T(8,128)} %get-tuple-element.36) | copy-start | bytes 73732
  34.8 83.6 %collective-permute-start.6 = (f32[4,144,256]{2,1,0:T(8,128)}, f32[4,144,256]{2,1,0:T(8,128)S(1)}, u32[]{:S(2)}, u32[]{:S(2)}) collective-permute-start(f32[4,144,256]{2,1,0:T(8,128)} %get-tuple-element.39), channel_id=1, source_target_pairs={{0,1},{1,2},{2,3},{3,4},{4,5},{5,6},{6,7},{7,8},{8,9},{9,10},{10,1... | collective-permute-start | bytes 1769480 | tf_op jit(solution)/shard_map/ppermute | solution.py:902
  34.8 83.6 %collective-permute-start.7 = (f32[4,144,256]{2,1,0:T(8,128)}, f32[4,144,256]{2,1,0:T(8,128)S(1)}, u32[]{:S(2)}, u32[]{:S(2)}) collective-permute-start(f32[4,144,256]{2,1,0:T(8,128)} %get-tuple-element.40), channel_id=1, source_target_pairs={{0,15},{1,0},{2,1},{3,2},{4,3},{5,4},{6,5},{7,6},{8,7},{9,8},{10,9... | collective-permute-start | bytes 1769480 | tf_op jit(solution)/shard_map/ppermute | solution.py:902
  40.9 3.3 %collective-permute-start.5 = (f32[48,128]{1,0:T(8,128)S(1)}, f32[48,128]{1,0:T(8,128)S(1)}, u32[]{:S(2)}, u32[]{:S(2)}) collective-permute-start(f32[48,128]{1,0:T(8,128)S(1)} %slice_bitcast_fusion), channel_id=1, source_target_pairs={{0,16},{16,32},{32,48},{48,64},{64,80},{80,96},{96,112},{112,0},{1... | collective-permute-start | bytes 73736 | tf_op jit(solution)/shard_map/ppermute | solution.py:902
  40.9 11.6 %collective-permute-start.4 = (f32[48,128]{1,0:T(8,128)S(1)}, f32[48,128]{1,0:T(8,128)S(1)}, u32[]{:S(2)}, u32[]{:S(2)}) collective-permute-start(f32[48,128]{1,0:T(8,128)S(1)} %copy-done.10), channel_id=1, source_target_pairs={{0,1},{1,2},{2,3},{3,4},{4,5},{5,6},{6,7},{7,8},{8,9},{9,10},{10,1... | collective-permute-start | bytes 73736 | tf_op jit(solution)/shard_map/ppermute | solution.py:902
  44.1 8.4 %copy-start.4 = (f32[48,128]{1,0:T(8,128)}, f32[48,128]{1,0:T(8,128)S(1)}, u32[]{:S(2)}) copy-start(f32[48,128]{1,0:T(8,128)S(1)} %collective-permute-done.5.row_ref) | copy-start | bytes 73732
  52.5 0.6 copy-start.5
  118.4 0.8 copy-start
  118.4 1.0 copy-start.1
